TPU v7x, 128 devices: a whole 4x4x4 slice. The times are simulated.
128 devices in a mesh: grp: 2 (over y_lo), dev: 64 (over y_hi, x, z, core).
Axes of the slice: x: 4, y: 4 (y_hi: 2, y_lo: 2; y = y_hi * 2 + y_lo), z: 4, core: 2. Of those that a mesh axis runs over, the one named last changes fastest.
Arguments:
- weights: float32 [2, 64, 524288], P(None, None, ('grp', 'dev')), may hold values from -3 to 3
- owner_map: int32 [16], replicated, may hold values from 0 to 15, each once
- node_index: int32 [2, 64], replicated, may hold values from 0 to 7, as said below
Outputs:
- transformed: float32 [2, 64, 524288], P(None, None, ('grp', 'dev'))
Inputs may be any that keep to these rules, and one draw needn't show every extreme that they name: owner_map[col] = 2 k + rx puts coarse frequency column col at column slot rx of device group k, in grp+dev order, after the middle level; every value appears once. The 64 columns (node_index[0, t], node_index[1, t]) are distinct, so every pair of Chebyshev point numbers appears once.
All inputs are finite; a program needn't handle non-finite values.
Results may differ from a plain program's by a relative error of at most 0.0003.
Values sent between devices are 32-bit elements; how exact they have to be, the bound alone decides.
A program may use at most 128 MiB of HBM per device.

v0:
```python
import math

import jax
import jax.numpy as jnp
from jax import lax
from jax.sharding import PartitionSpec as P

NFREQ = 4096
CHEB = 8


TWO_PI = 2.0 * math.pi
HIGHEST = lax.Precision.HIGHEST


def from_partner(array, axis, bit):
    return lax.ppermute(array, axis, [(i, i ^ 1 << bit) for i in range(lax.axis_size(axis))])


def cheb_points():
    counter = jnp.arange(CHEB, dtype=jnp.float32)
    return 0.5 * jnp.cos(math.pi * (2.0 * counter + 1.0) / (2.0 * CHEB))


def node_select(node_index):
    numbers = jnp.arange(CHEB, dtype=jnp.int32)[None, :]
    select_x = (node_index[0][:, None] == numbers).astype(jnp.float32)
    select_y = (node_index[1][:, None] == numbers).astype(jnp.float32)
    return (select_x, select_y)


def node_offsets(node_index):
    points = cheb_points()
    select_x, select_y = node_select(node_index)
    return (
        jnp.sum(select_x * points[None, :], axis=1),
        jnp.sum(select_y * points[None, :], axis=1),
    )


def lagrange(places):
    points = cheb_points()
    rows_out = []
    for first_id in range(CHEB):
        product = jnp.ones_like(places)
        for other_id in range(CHEB):
            if other_id != first_id:
                product = (
                    product * (places - points[other_id]) / (points[first_id] - points[other_id])
                )
        rows_out.append(product)
    return jnp.stack(rows_out)


def child_tables(node_index):
    select_x, select_y = node_select(node_index)
    offset_x, offset_y = node_offsets(node_index)
    tables = []
    for child_id in range(4):
        basis_x = lagrange(0.5 * offset_x + 0.5 * (child_id % 2) - 0.25)
        basis_y = lagrange(0.5 * offset_y + 0.5 * (child_id // 2) - 0.25)
        table_x = jnp.sum(select_x[:, :, None] * basis_x[None, :, :], axis=1)
        table_y = jnp.sum(select_y[:, :, None] * basis_y[None, :, :], axis=1)
        tables.append(table_x * table_y)
    return jnp.stack(tables)


def speeds(place_x, place_y):
    speed_one = (2.0 + jnp.sin(TWO_PI * place_x) * jnp.sin(TWO_PI * place_y)) / 16.0
    speed_two = (2.0 + jnp.cos(TWO_PI * place_x) * jnp.cos(TWO_PI * place_y)) / 16.0
    return (speed_one * speed_one, speed_two * speed_two)


def radius(speed_x, speed_y, freq_x, freq_y):
    return jnp.sqrt(speed_x * freq_x * freq_x + speed_y * freq_y * freq_y + 1.0)


def freq_phase(place_x, place_y, freq_x, freq_y, centre_x, centre_y):
    speed_x, speed_y = speeds(place_x, place_y)
    numer_part = speed_x * (freq_x - centre_x) * (freq_x + centre_x) + speed_y * (
        freq_y - centre_y
    ) * (freq_y + centre_y)
    denom_part = radius(speed_x, speed_y, freq_x, freq_y) + radius(
        speed_x, speed_y, centre_x, centre_y
    )
    return TWO_PI * (
        place_x * (freq_x - centre_x) + place_y * (freq_y - centre_y) + numer_part / denom_part
    )


def space_phase(place_x, place_y, anchor_x, anchor_y, freq_x, freq_y):
    speed_x, speed_y = speeds(place_x, place_y)
    base_x, base_y = speeds(anchor_x, anchor_y)
    numer_part = (speed_x - base_x) * freq_x * freq_x + (speed_y - base_y) * freq_y * freq_y
    denom_part = radius(speed_x, speed_y, freq_x, freq_y) + radius(base_x, base_y, freq_x, freq_y)
    return TWO_PI * (
        (place_x - anchor_x) * freq_x + (place_y - anchor_y) * freq_y + numer_part / denom_part
    )


def rotate(values, phase_angle):
    cosine = jnp.cos(phase_angle)
    sine_part = jnp.sin(phase_angle)
    return jnp.stack(
        [values[0] * cosine - values[1] * sine_part, values[0] * sine_part + values[1] * cosine]
    )


def freq_level(pieces, space_x, space_y, box_x, box_y, level_id, offset_x, offset_y):
    width_a = 2.0 ** (-level_id)
    width_b = 2.0**level_id
    half_span = 0.5 * NFREQ
    centre_ax = ((space_x + 0.5) * width_a)[None, :]
    centre_ay = ((space_y + 0.5) * width_a)[None, :]
    centre_bx = ((box_x + 0.5) * width_b - half_span)[None, :]
    centre_by = ((box_y + 0.5) * width_b - half_span)[None, :]
    running = None
    for values, child_x, child_y, table_now in pieces:
        kid_x = ((2.0 * box_x + child_x + 0.5) * (0.5 * width_b) - half_span)[
            None, :
        ] + 0.5 * width_b * offset_x[:, None]
        kid_y = ((2.0 * box_y + child_y + 0.5) * (0.5 * width_b) - half_span)[
            None, :
        ] + 0.5 * width_b * offset_y[:, None]
        phase_angle = freq_phase(centre_ax, centre_ay, kid_x, kid_y, centre_bx, centre_by)
        product_term = jnp.einsum(
            "ts,rsn->rtn", table_now, rotate(values, -phase_angle), precision=HIGHEST
        )
        running = product_term if running is None else running + product_term
    node_x = centre_bx + width_b * offset_x[:, None]
    node_y = centre_by + width_b * offset_y[:, None]
    return rotate(running, freq_phase(centre_ax, centre_ay, node_x, node_y, centre_bx, centre_by))


def space_in(values, offset_x, offset_y, parent_x, parent_y, box_x, box_y, level_id):
    width_p = 2.0 ** (1 - level_id)
    anchor_x = ((parent_x + 0.5) * width_p)[None, :]
    anchor_y = ((parent_y + 0.5) * width_p)[None, :]
    freq_x = ((box_x + 0.5) * 2.0**level_id - 0.5 * NFREQ)[None, :]
    freq_y = ((box_y + 0.5) * 2.0**level_id - 0.5 * NFREQ)[None, :]
    place_x = anchor_x + width_p * offset_x[:, None]
    place_y = anchor_y + width_p * offset_y[:, None]
    return rotate(values, -space_phase(place_x, place_y, anchor_x, anchor_y, freq_x, freq_y))


def space_out(
    turned_in,
    table_now,
    offset_x,
    offset_y,
    parent_x,
    parent_y,
    child_x,
    child_y,
    box_x,
    box_y,
    level_id,
):
    width_a = 2.0 ** (-level_id)
    mixed_state = jnp.einsum("st,rsn->rtn", table_now, turned_in, precision=HIGHEST)
    anchor_x = ((parent_x + 0.5) * 2.0 * width_a)[None, :]
    anchor_y = ((parent_y + 0.5) * 2.0 * width_a)[None, :]
    place_x = ((2.0 * parent_x + child_x + 0.5) * width_a)[None, :] + width_a * offset_x[:, None]
    place_y = ((2.0 * parent_y + child_y + 0.5) * width_a)[None, :] + width_a * offset_y[:, None]
    freq_x = ((box_x + 0.5) * 2.0**level_id - 0.5 * NFREQ)[None, :]
    freq_y = ((box_y + 0.5) * 2.0**level_id - 0.5 * NFREQ)[None, :]
    return rotate(mixed_state, space_phase(place_x, place_y, anchor_x, anchor_y, freq_x, freq_y))


def first_geometry(step_id, group_ids, low_digit, high_digit, loc_ids, across):
    column = loc_ids % across
    row_id = loc_ids // across
    if step_id == 0:
        space_x = 2 * group_ids + low_digit % 2
        space_y = low_digit // 2
        box_x = 2 * column + high_digit % 2
        box_y = 2 * row_id + high_digit // 2
    else:
        space_x = 4 * group_ids + 2 * (low_digit % 2) + high_digit % 2
        space_y = 2 * (low_digit // 2) + high_digit // 2
        box_x = column
        box_y = row_id
    return [
        jnp.broadcast_to(jnp.asarray(entry_value), loc_ids.shape).astype(jnp.float32)
        for entry_value in (space_x, space_y, box_x, box_y)
    ]


def post_layout(loc_ids, per_source, rest_rows):
    source = loc_ids // per_source
    remain = loc_ids % per_source
    rest_x = remain // rest_rows
    rest_y = remain % rest_rows
    src_group = source // 16
    src_digits = source % 16
    low_digit = src_digits % 4
    high_digit = src_digits // 4
    middle_x = 4 * src_group + 2 * (low_digit % 2) + high_digit % 2
    middle_y = 2 * (low_digit // 2) + high_digit // 2
    return (middle_x, middle_y, rest_x, rest_y)


def second_geometry(step_id, middle_x, middle_y, column, rest_y, other_digit):
    if step_id == 0:
        parent_x = middle_x
        parent_y = middle_y
        box_x = 2 * column + other_digit % 2
        box_y = 2 * rest_y + other_digit // 2
    else:
        parent_x = 2 * middle_x + other_digit % 2
        parent_y = 2 * middle_y + other_digit // 2
        box_x = column
        box_y = rest_y
    return [
        jnp.asarray(entry_value).astype(jnp.float32)
        for entry_value in (parent_x, parent_y, box_x, box_y)
    ]


def owner_inverse(owner_map, count):
    counter = jnp.arange(count, dtype=jnp.int32)
    return jnp.sum(jnp.where(owner_map[None, :] == counter[:, None], counter[None, :], 0), axis=1)


def finish_levels(pair_state, owner_map, tables, offset_x, offset_y, first_level, across):
    node_count = pair_state.shape[1]
    per_dev = pair_state.shape[2]
    dev_count = lax.axis_size("dev")
    grp_count = lax.axis_size("grp")
    devices = dev_count * grp_count
    groups = devices // 16
    per_source = per_dev // devices
    rest_rows = per_dev // across // 4
    group_width = across // 4 // groups
    grp_index = lax.axis_index("grp")
    dev_index = lax.axis_index("dev")
    flat_index = grp_index * dev_count + dev_index
    own_group = flat_index // 16
    own_digits = flat_index % 16
    loc_index = jnp.arange(per_dev, dtype=jnp.int32)
    inverse = owner_inverse(owner_map, 16)
    blocks = pair_state.reshape(2, node_count, rest_rows, 2, 2, 16, 2, 2)
    blocks = jnp.transpose(blocks, (0, 1, 5, 3, 6, 4, 7, 2))
    blocks = jnp.take(blocks, inverse, axis=2)
    blocks = blocks.reshape(2, node_count, groups, group_width, 2, 2, 2, 2, rest_rows)
    blocks = jnp.transpose(blocks, (0, 1, 2, 4, 5, 6, 7, 3, 8))
    pair_state = lax.all_to_all(
        blocks.reshape(2, node_count, devices, per_source),
        ("grp", "dev"),
        split_axis=2,
        concat_axis=2,
        tiled=True,
    ).reshape(2, node_count, per_dev)
    middle_x, middle_y, rest_x, rest_y = post_layout(loc_index, per_source, rest_rows)
    column = jnp.take(inverse, own_group * group_width + rest_x)
    for step_id in range(2):
        if step_id == 0:
            own_digit = own_digits % 4
            other_digit = own_digits // 4
        else:
            own_digit = own_digits // 4
            other_digit = own_digits % 4
        level_id = first_level + 3 + step_id
        geometry = second_geometry(step_id, middle_x, middle_y, column, rest_y, other_digit)
        pair_sum = pair_state + from_partner(pair_state, "dev", 2 * step_id)
        summed = pair_sum + from_partner(pair_sum, "dev", 2 * step_id + 1)
        turned_in = space_in(
            summed, offset_x, offset_y, geometry[0], geometry[1], geometry[2], geometry[3], level_id
        )
        table_own = lax.dynamic_index_in_dim(tables, own_digit, 0, keepdims=False)
        pair_state = space_out(
            turned_in,
            table_own,
            offset_x,
            offset_y,
            geometry[0],
            geometry[1],
            (own_digit % 2).astype(jnp.float32),
            (own_digit // 2).astype(jnp.float32),
            geometry[2],
            geometry[3],
            level_id,
        )
    return pair_state


def body(weights, owner_map, node_index):
    per_dev = weights.shape[2]
    dev_count = lax.axis_size("dev")
    levels = NFREQ.bit_length() - 1
    first_level = levels // 2 - 2
    across = 2 ** (levels // 2)
    offset_x, offset_y = node_offsets(node_index)
    tables = child_tables(node_index)
    grp_index = lax.axis_index("grp")
    dev_index = lax.axis_index("dev")
    flat_index = grp_index * dev_count + dev_index
    own_group = flat_index // 16
    own_digits = flat_index % 16
    loc_index = jnp.arange(per_dev, dtype=jnp.int32)
    pair_state = weights
    for step_id in range(2):
        if step_id == 0:
            own_digit = own_digits % 4
            low_digit = own_digit
            high_digit = own_digits // 4
        else:
            own_digit = own_digits // 4
            low_digit = own_digits % 4
            high_digit = own_digit
        near_state = from_partner(pair_state, "dev", 2 * step_id)
        far_one, far_two = from_partner((pair_state, near_state), "dev", 2 * step_id + 1)
        arrived = [pair_state, near_state, far_one, far_two]
        pieces = []
        for delta_id in range(4):
            child_id = jnp.bitwise_xor(own_digit, delta_id)
            pieces.append(
                (
                    arrived[delta_id],
                    (child_id % 2).astype(jnp.float32),
                    (child_id // 2).astype(jnp.float32),
                    lax.dynamic_index_in_dim(tables, child_id, 0, keepdims=False),
                )
            )
        geometry = first_geometry(step_id, own_group, low_digit, high_digit, loc_index, across)
        pair_state = freq_level(
            pieces,
            geometry[0],
            geometry[1],
            geometry[2],
            geometry[3],
            first_level + 1 + step_id,
            offset_x,
            offset_y,
        )
    pair_state = finish_levels(
        pair_state, owner_map, tables, offset_x, offset_y, first_level, across
    )
    return pair_state


def solution(mesh):
    in_specs = (P(None, None, ("grp", "dev")), P(), P())
    out_specs = P(None, None, ("grp", "dev"))
    return jax.shard_map(body, mesh=mesh, in_specs=in_specs, out_specs=out_specs, check_vma=False)
```

profile of v0, /device:TPU:1, one launch (start us, length us, event | category | flops | bytes accessed | tf_op | source)
XLA Modules:
  0.0 571.5 jit_solution(14105891888162504395)
XLA Ops:
  84.7 6.3 %multiply_subtract_fusion.13 = (f32[1,64,4096]{2,1,0:T(8,128)S(1)}, f32[1,64,4096]{2,1,0:T(8,128)S(1)}) fusion(f32[2,64,4096]{2,1,0:T(8,128)} %param.3, f32[4096]{0:T(1024)S(1)} %get-tuple-element.154, f32[]{:T(128)S(6)} %mul.7297, f32[]{:T(128)S(6)} %mul.7291, f32[4096]{0:T(1024)S(1)} %fusion.362, f32[64]{0:T(128)S(1)} %get-tuple-element.115, ...), kind=kLoop, calls=%fused_computation.399 | loop fusion | flops 8126464 | bytes 4276752 | tf_op jit(solution)/shard_map/sub | solution.py:105
  93.5 5.1 multiply_subtract_fusion.12
  100.6 6.8 %multiply_subtract_fusion.11 = (f32[1,64,4096]{2,1,0:T(8,128)S(1)}, f32[1,64,4096]{2,1,0:T(8,128)S(1)}) fusion(f32[2,64,4096]{2,1,0:T(8,128)} %collective-permute-done.1, f32[4096]{0:T(1024)S(1)} %get-tuple-element.154, f32[]{:T(128)S(6)} %mul.7297, f32[]{:T(128)S(6)} %mul.7291, f32[4096]{0:T(1024)S(1)} %fusion.362, f32[64]{0:T(128)S(1)} %get-tuple-element.115, ...), kind=kLoop, calls=%fused_computation.395 | loop fusion | flops 8126464 | bytes 4276752 | tf_op jit(solution)/shard_map/sub | solution.py:105
  109.5 30.8 %collective-permute-done.2 = f32[2,64,4096]{2,1,0:T(8,128)S(1)} collective-permute-done((f32[2,64,4096]{2,1,0:T(8,128)S(1)}, f32[2,64,4096]{2,1,0:T(8,128)S(1)}, u32[]{:S(2)}, u32[]{:S(2)}) %collective-permute-start.2) | collective-permute-done | bytes 2097184 | tf_op jit(solution)/shard_map/ppermute | solution.py:17
  140.4 5.1 multiply_subtract_fusion.10
  147.5 10.1 %multiply_subtract_fusion.8 = (f32[1,64,4096]{2,1,0:T(8,128)S(1)}, f32[1,64,4096]{2,1,0:T(8,128)S(1)}, f32[1,64,4096]{2,1,0:T(8,128)S(1)}) fusion(f32[4096]{0:T(1024)S(1)} %get-tuple-element.195, f32[]{:T(128)S(6)} %mul.7617, f32[]{:T(128)S(6)} %mul.7611, f32[4096]{0:T(1024)S(1)} %get-tuple-element.194, f32[64]{0:T(128)S(1)} %get-tuple-element.114, ...), kind=kLoop, calls=%fused_computation.389 | loop fusion | flops 15204352 | bytes 5374496 | tf_op jit(solution)/shard_map/sub | solution.py:105
  163.9 43.7 %collective-permute-done.3 = f32[2,64,4096]{2,1,0:T(8,128)} collective-permute-done((f32[2,64,4096]{2,1,0:T(8,128)}, f32[2,64,4096]{2,1,0:T(8,128)}, u32[]{:S(2)}, u32[]{:S(2)}) %collective-permute-start.3) | collective-permute-done | bytes 2097184 | tf_op jit(solution)/shard_map/ppermute | solution.py:17
  208.9 6.3 %multiply_subtract_fusion.7 = (f32[1,64,4096]{2,1,0:T(8,128)S(1)}, f32[1,64,4096]{2,1,0:T(8,128)S(1)}) fusion(f32[2,64,4096]{2,1,0:T(8,128)} %collective-permute-done.3, f32[4096]{0:T(1024)S(1)} %get-tuple-element.195, f32[]{:T(128)S(6)} %mul.7617, f32[]{:T(128)S(6)} %mul.7611, f32[4096]{0:T(1024)S(1)} %get-tuple-element.194, f32[64]{0:T(128)S(1)} %get-tuple-element.114, ...), kind=kLoop, calls=%fused_computation.387 | loop fusion | flops 8126464 | bytes 4276752 | tf_op jit(solution)/shard_map/sub | solution.py:105
  215.2 6.3 %multiply_subtract_fusion.6 = (f32[1,64,4096]{2,1,0:T(8,128)S(1)}, f32[1,64,4096]{2,1,0:T(8,128)S(1)}) fusion(f32[2,64,4096]{2,1,0:T(8,128)} %collective-permute-done.4, f32[4096]{0:T(1024)S(1)} %get-tuple-element.195, f32[]{:T(128)S(6)} %mul.7617, f32[]{:T(128)S(6)} %mul.7611, f32[4096]{0:T(1024)S(1)} %get-tuple-element.194, f32[64]{0:T(128)S(1)} %get-tuple-element.114, ...), kind=kLoop, calls=%fused_computation.385 | loop fusion | flops 8126464 | bytes 4276752 | tf_op jit(solution)/shard_map/sub | solution.py:105
  221.5 31.9 %collective-permute-done.5 = f32[2,64,4096]{2,1,0:T(8,128)} collective-permute-done((f32[2,64,4096]{2,1,0:T(8,128)}, f32[2,64,4096]{2,1,0:T(8,128)}, u32[]{:S(2)}, u32[]{:S(2)}) %collective-permute-start.5) | collective-permute-done | bytes 2097184 | tf_op jit(solution)/shard_map/ppermute | solution.py:17
  253.4 11.4 %multiply_subtract_fusion.5 = (f32[1,64,4096]{2,1,0:T(8,128)S(1)}, f32[1,64,4096]{2,1,0:T(8,128)S(1)}, f32[1,64,4096]{2,1,0:T(8,128)S(1)}) fusion(f32[2,64,4096]{2,1,0:T(8,128)} %collective-permute-done.5, f32[4096]{0:T(1024)S(1)} %get-tuple-element.195, f32[]{:T(128)S(6)} %mul.7617, f32[]{:T(128)S(6)} %mul.7611, f32[4096]{0:T(1024)S(1)} %get-tuple-element.194, ...), kind=kLoop, calls=%fused_computation.383 | loop fusion | flops 15466496 | bytes 7455248 | tf_op jit(solution)/shard_map/sub | solution.py:105
  273.0 6.4 %multiply_subtract_fusion.4 = (f32[1,64,4096]{2,1,0:T(8,128)}, f32[1,64,4096]{2,1,0:T(8,128)S(1)}) fusion(f32[2,64,4096]{2,1,0:T(8,128)S(1)} %fusion, f32[4096]{0:T(1024)S(1)} %get-tuple-element.195, f32[]{:T(128)S(6)} %mul.7617, f32[]{:T(128)S(6)} %mul.7611, f32[64]{0:T(128)S(1)} %get-tuple-element.116, f32[4096]{0:T(1024)S(1)} %get-tuple-element.194, ...), kind=kLoop, calls=%fused_computation.381 | loop fusion | flops 7864320 | bytes 4243984 | tf_op jit(solution)/shard_map/sub | solution.py:105
  288.4 5.0 gather_fusion
  303.4 42.1 %all_to_all.5 = f32[128,1,4096]{2,1,0:T(1,128)} all-to-all(f32[128,1,4096]{2,1,0:T(1,128)S(1)} %reshape.12153), channel_id=1, replica_groups=mesh['grp'=2,'dev'=64] {'grp','dev'}, dimensions={0} | all-to-all | bytes 4194304 | tf_op jit(solution)/shard_map/all_to_all | solution.py:247
  346.0 7.3 %reduce.18 = f32[128,4096]{1,0:T(8,128)S(1)} reduce(f32[128,1,4096]{2,1,0:T(1,128)} %all_to_all.5, f32[]{:T(128)} %broadcast.18834), dimensions={1}, to_apply=%all_to_all.3.reduce_sub_computation | reduce | bytes 4194308 | tf_op jit(solution)/shard_map/all_to_all | solution.py:247
  356.3 4.7 copy.35
  375.9 5.7 multiply_add_fusion.16
  382.0 33.9 %collective-permute-done.7 = f32[2,64,4096]{2,1,0:T(8,128)S(1)} collective-permute-done((f32[2,64,4096]{2,1,0:T(8,128)S(1)}, f32[2,64,4096]{2,1,0:T(8,128)S(1)}, u32[]{:S(2)}, u32[]{:S(2)}) %collective-permute-start.7) | collective-permute-done | bytes 2097184 | tf_op jit(solution)/shard_map/ppermute | solution.py:17
  416.1 13.1 %multiply_subtract_fusion.3 = (f32[1,64,4096]{2,1,0:T(8,128)S(1)}, f32[1,64,4096]{2,1,0:T(8,128)S(1)}) fusion(f32[2,64,4096]{2,1,0:T(8,128)S(1)} %add.5384, f32[4096]{0:T(1024)S(1)} %get-tuple-element.13, f32[4096]{0:T(1024)S(1)} %get-tuple-element.203, f32[4096]{0:T(1024)S(1)} %get-tuple-element.204, f32[4096]{0:T(1024)S(1)} %get-tuple-element.158, ...), kind=kLoop, calls=%fused_computation.379 | loop fusion | flops 10747904 | bytes 4309504 | tf_op jit(solution)/shard_map/sub | solution.py:105
  431.2 12.9 %multiply_subtract_fusion.2 = (f32[1,64,4096]{2,1,0:T(8,128)S(1)}, f32[1,64,4096]{2,1,0:T(8,128)S(1)}) fusion(f32[2,64,4096]{2,1,0:T(8,128)S(1)} %convolution_bitcast_fusion.1, f32[4096]{0:T(1024)S(1)} %get-tuple-element.13, f32[4096]{0:T(1024)S(1)} %get-tuple-element.203, f32[4096]{0:T(1024)S(1)} %get-tuple-element.204, f32[4096]{0:T(1024)S(1)} %get-tuple-element.158, ...), kind=kLoop, calls=%fused_computation.377 | loop fusion | flops 10485760 | bytes 4342272 | tf_op jit(solution)/shard_map/sub | solution.py:105
  444.8 47.0 %collective-permute-done.8 = f32[2,64,4096]{2,1,0:T(8,128)S(1)} collective-permute-done((f32[2,64,4096]{2,1,0:T(8,128)S(1)}, f32[2,64,4096]{2,1,0:T(8,128)S(1)}, u32[]{:S(2)}, u32[]{:S(2)}) %collective-permute-start.8) | collective-permute-done | bytes 2097184 | tf_op jit(solution)/shard_map/ppermute | solution.py:17
  494.3 45.1 %collective-permute-done.9 = f32[2,64,4096]{2,1,0:T(8,128)} collective-permute-done((f32[2,64,4096]{2,1,0:T(8,128)}, f32[2,64,4096]{2,1,0:T(8,128)}, u32[]{:S(2)}, u32[]{:S(2)}) %collective-permute-start.9) | collective-permute-done | bytes 2097184 | tf_op jit(solution)/shard_map/ppermute | solution.py:17
  542.0 13.1 %multiply_subtract_fusion.1 = (f32[1,64,4096]{2,1,0:T(8,128)S(1)}, f32[1,64,4096]{2,1,0:T(8,128)S(1)}) fusion(f32[2,64,4096]{2,1,0:T(8,128)S(1)} %fusion.460, f32[4096]{0:T(1024)S(1)} %get-tuple-element.87, f32[4096]{0:T(1024)S(1)} %get-tuple-element.152, f32[4096]{0:T(1024)S(1)} %get-tuple-element.153, f32[4096]{0:T(1024)S(1)} %multiply_add_fusion.14, ...), kind=kLoop, calls=%fused_computation.375 | loop fusion | flops 10747904 | bytes 4309504 | tf_op jit(solution)/shard_map/sub | solution.py:105
  557.1 12.9 %multiply_subtract_fusion = (f32[2,64,4096]{2,1,0:T(8,128)S(1)}, f32[2,64,4096]{2,1,0:T(8,128)S(1)}) fusion(f32[2,64,4096]{2,1,0:T(8,128)S(1)} %convolution_bitcast_fusion, f32[4096]{0:T(1024)S(1)} %get-tuple-element.87, f32[4096]{0:T(1024)S(1)} %get-tuple-element.152, ...), kind=kLoop, output_to_operand_aliasing={{0}: (12, {}), {1}: (12, {})}, calls=%fused_computation.373 | loop fusion | flops 10485760 | bytes 4342784 | tf_op jit(solution)/shard_map/sub | solution.py:105
  (132 shorter events, 86.5 us)
Async XLA Ops:
  0.0 93.1 %collective-permute-start = (f32[2,64,4096]{2,1,0:T(8,128)}, f32[2,64,4096]{2,1,0:T(8,128)S(1)}, u32[]{:S(2)}, u32[]{:S(2)}) collective-permute-start(f32[2,64,4096]{2,1,0:T(8,128)} %param.3), channel_id=1, source_target_pairs={{0,1},{1,0},{2,3},{3,2},{4,5},{5,4},{6,7},{7,6},{8,9},{9,8},{10,11... | collective-permute-start | bytes 6291464 | tf_op jit(solution)/shard_map/ppermute | solution.py:17
  1.4 99.2 %collective-permute-start.1 = (f32[2,64,4096]{2,1,0:T(8,128)}, f32[2,64,4096]{2,1,0:T(8,128)}, u32[]{:S(2)}, u32[]{:S(2)}) collective-permute-start(f32[2,64,4096]{2,1,0:T(8,128)} %param.3), channel_id=1, source_target_pairs={{0,2},{1,3},{2,0},{3,1},{4,6},{5,7},{6,4},{7,5},{8,10},{9,11},{10,... | collective-permute-start | bytes 6291464 | tf_op jit(solution)/shard_map/ppermute | solution.py:17
  93.1 47.3 %collective-permute-start.2 = (f32[2,64,4096]{2,1,0:T(8,128)S(1)}, f32[2,64,4096]{2,1,0:T(8,128)S(1)}, u32[]{:S(2)}, u32[]{:S(2)}) collective-permute-start(f32[2,64,4096]{2,1,0:T(8,128)S(1)} %collective-permute-done), channel_id=1, source_target_pairs={{0,2},{1,3},{2,0},{3,1},{4,6},{5,7},{6,4},{7,5},{8,10},{9,11},{10,... | collective-permute-start | bytes 6291464 | tf_op jit(solution)/shard_map/ppermute | solution.py:17
  157.6 6.0 %copy-start.4 = (s32[16]{0:T(128)S(1)}, s32[16]{0:T(128)}, u32[]{:S(2)}) copy-start(s32[16]{0:T(128)} %param.4) | copy-start | bytes 196
  159.1 48.5 %collective-permute-start.3 = (f32[2,64,4096]{2,1,0:T(8,128)}, f32[2,64,4096]{2,1,0:T(8,128)}, u32[]{:S(2)}, u32[]{:S(2)}) collective-permute-start(f32[2,64,4096]{2,1,0:T(8,128)} %pad_maximum_fusion), channel_id=1, source_target_pairs={{0,4},{1,5},{2,6},{3,7},{4,0},{5,1},{6,2},{7,3},{8,12},{9,13},{10,... | collective-permute-start | bytes 6291464 | tf_op jit(solution)/shard_map/ppermute | solution.py:17
  162.4 52.8 %collective-permute-start.4 = (f32[2,64,4096]{2,1,0:T(8,128)}, f32[2,64,4096]{2,1,0:T(8,128)}, u32[]{:S(2)}, u32[]{:S(2)}) collective-permute-start(f32[2,64,4096]{2,1,0:T(8,128)} %pad_maximum_fusion), channel_id=1, source_target_pairs={{0,8},{1,9},{2,10},{3,11},{4,12},{5,13},{6,14},{7,15},{8,0},{9,1},... | collective-permute-start | bytes 6291464 | tf_op jit(solution)/shard_map/ppermute | solution.py:17
  207.6 45.8 %collective-permute-start.5 = (f32[2,64,4096]{2,1,0:T(8,128)}, f32[2,64,4096]{2,1,0:T(8,128)}, u32[]{:S(2)}, u32[]{:S(2)}) collective-permute-start(f32[2,64,4096]{2,1,0:T(8,128)} %collective-permute-done.3), channel_id=1, source_target_pairs={{0,8},{1,9},{2,10},{3,11},{4,12},{5,13},{6,14},{7,15},{8,0},{9,1},... | collective-permute-start | bytes 6291464 | tf_op jit(solution)/shard_map/ppermute | solution.py:17
  284.3 1.6 copy-start.1
  363.9 4.6 collective-permute-start.6
  368.8 47.1 %collective-permute-start.7 = (f32[2,64,4096]{2,1,0:T(8,128)S(1)}, f32[2,64,4096]{2,1,0:T(8,128)S(1)}, u32[]{:S(2)}, u32[]{:S(2)}) collective-permute-start(f32[2,64,4096]{2,1,0:T(8,128)S(1)} %add.5383), channel_id=1, source_target_pairs={{0,2},{1,3},{2,0},{3,1},{4,6},{5,7},{6,4},{7,5},{8,10},{9,11},{10,... | collective-permute-start | bytes 6291464 | tf_op jit(solution)/shard_map/ppermute | solution.py:17
  444.3 47.5 %collective-permute-start.8 = (f32[2,64,4096]{2,1,0:T(8,128)S(1)}, f32[2,64,4096]{2,1,0:T(8,128)S(1)}, u32[]{:S(2)}, u32[]{:S(2)}) collective-permute-start(f32[2,64,4096]{2,1,0:T(8,128)S(1)} %pad_maximum_fusion.1), channel_id=1, source_target_pairs={{0,4},{1,5},{2,6},{3,7},{4,0},{5,1},{6,2},{7,3},{8,12},{9,13},{10,... | collective-permute-start | bytes 6291464 | tf_op jit(solution)/shard_map/ppermute | solution.py:17
  491.8 2.0 copy-start
  493.8 45.6 %collective-permute-start.9 = (f32[2,64,4096]{2,1,0:T(8,128)}, f32[2,64,4096]{2,1,0:T(8,128)}, u32[]{:S(2)}, u32[]{:S(2)}) collective-permute-start(f32[2,64,4096]{2,1,0:T(8,128)} %fusion.457), channel_id=1, source_target_pairs={{0,8},{1,9},{2,10},{3,11},{4,12},{5,13},{6,14},{7,15},{8,0},{9,1},... | collective-permute-start | bytes 6291464 | tf_op jit(solution)/shard_map/ppermute | solution.py:17
  555.1 2.0 copy-start.2
  570.0 1.3 copy-start.3
where the time goes:
time: 580 us; the launch traced here: 571 us
  waiting for transfers between devices  236 us (41%)
  other arithmetic  156 us (27%)
  between operations  72 us (12%)
  blocking collectives  42.1 us (7%)
  local copies, waits for them, and re-layouts  33.8 us (6%)
  matrix products  20.4 us (4%)
  starting transfers between devices  11.4 us (2%)
    ppermute x10, waiting for transfers between devices, from_partner(): lax.ppermute(array, axis, [(i, i ^ 1 << bit) for i in range(lax.axis_size...  236 us
    sub x14, other arithmetic, rotate(): values[0] * cosine - values[1] * sine_part  116 us
    all_to_all x1, blocking collectives, finish_levels(): lax.all_to_all(blocks.reshape(2, node_count, devices, per_source), ('grp'...  42.1 us
    dot_general x8, matrix products, freq_level(): jnp.einsum('ts,rsn->rtn', table_now, rotate(values, -phase_angle), precis...  16.4 us
  transfers between devices with their start and end apart: 10, of which 7 were waited for; matrix products, arithmetic and copies ran while one was open for 11% of the time, Pallas kernels for 0%

commit v1 on v0

v1 whole, which is shorter than its diff:
```python
import functools
import math

import jax
import jax.numpy as jnp
import numpy as np
from jax import lax
from jax.experimental import pallas as pl
from jax.experimental.pallas import tpu as pltpu
from jax.sharding import PartitionSpec as P

F32 = jnp.float32
BF16 = jnp.bfloat16
HALF = 2048.0
NT_DIMS = (((1,), (1,)), ((), ()))
TN_DIMS = (((0,), (0,)), ((), ()))
NN_DIMS = (((1,), (0,)), ((), ()))


def fit(function, count):
    angle = (np.arange(64) + 0.5) * np.pi / 64
    points = 0.125 + 0.125 * np.cos(angle)
    cheb = np.polynomial.chebyshev.Chebyshev.fit(
        points, function(np.sqrt(points)), count - 1, domain=[0.0, 0.25]
    )
    return [float(c) for c in cheb.convert(kind=np.polynomial.Polynomial).coef]


SIN_COEF = fit(lambda r: np.sin(np.pi * r) / r, 5)
COS_COEF = fit(lambda r: 2.0 * np.cos(np.pi * r), 6)


def horner(coef, u):
    total = coef[-1] * u + coef[-2]
    for c in coef[-3::-1]:
        total = total * u + c
    return total


def trig(cycles):
    r = cycles - jnp.round(cycles)
    u = r * r
    s = horner(SIN_COEF, u) * r
    c2 = horner(COS_COEF, u)
    return 1.0 - 2.0 * (s * s), s * c2


def cheb_nodes():
    return 0.5 * np.cos(np.pi * (2.0 * np.arange(8) + 1.0) / 16.0)


def canon_tables():
    z = cheb_nodes()
    basis = np.zeros((2, 8, 8))
    for c in range(2):
        places = z / 2 + c / 2 - 0.25
        for i in range(8):
            value = np.ones(8)
            for k in range(8):
                if k != i:
                    value = value * (places - z[k]) / (z[i] - z[k])
            basis[c, i] = value
    return [np.kron(basis[c % 2], basis[c // 2]) for c in range(4)]


def split_np(a):
    hi = np.asarray(a, np.float32).astype(BF16)
    lo = (np.asarray(a, np.float64) - hi.astype(np.float64)).astype(np.float32).astype(BF16)
    return hi, lo


def constants():
    z = cheb_nodes().astype(np.float32)
    tables = canon_tables()
    t_in = np.concatenate(tables, axis=1)
    t_out = np.concatenate([t.T for t in tables], axis=0)
    in_h, in_l = split_np(t_in)
    out_h, out_l = split_np(t_out)
    t1 = np.concatenate([in_h, in_l], axis=0)
    t3 = np.concatenate([out_h, out_h, out_l], axis=1)
    tf = np.stack([out_h, out_l])
    ox = np.repeat(z, 8)
    oy = np.tile(z, 8)
    off = np.stack([np.broadcast_to(o[:, None], (64, 128)) for o in (ox, oy)])
    pieces = []
    rest = off.astype(np.float32)
    for _ in range(3):
        piece = rest.astype(BF16)
        pieces.append(piece)
        rest = rest - piece.astype(np.float32)
    return t1, t3, tf, np.ascontiguousarray(off, np.float32), np.stack(pieces)


def fiota(shape, axis):
    return lax.broadcasted_iota(jnp.int32, shape, axis)


def node_onehot(node_ref):
    flat = node_ref[0:1, :] * 8 + node_ref[1:2, :]
    return (fiota((64, 64), 0) == flat).astype(F32).astype(BF16)


def dot(a, b, dims=NN_DIMS):
    return lax.dot_general(a, b, dims, preferred_element_type=F32)


def split(x):
    hi = x.astype(BF16)
    return hi, (x - hi.astype(F32)).astype(BF16)


def speeds(x1, x2):
    c1, s1 = trig(x1)
    c2, s2 = trig(x2)
    one = (2.0 + s1 * s2) * 0.0625
    two = (2.0 + c1 * c2) * 0.0625
    return one * one, two * two


def freq_cycles(d1, d2, g1, g2, a1, a2, v1, v2):
    numer = v1 * d1 * (2.0 * g1 + d1) + v2 * d2 * (2.0 * g2 + d2)
    square = v1 * g1 * g1 + v2 * g2 * g2 + 1.0
    denom = jnp.sqrt(square + numer) + jnp.sqrt(square)
    return a1 * d1 + a2 * d2 + numer / denom


def space_cycles(d1, d2, p1, p2, v1, v2, w1, w2, f1, f2):
    q1 = f1 * f1
    q2 = f2 * f2
    base = w1 * q1 + w2 * q2 + 1.0
    numer = (v1 - w1) * q1 + (v2 - w2) * q2
    denom = jnp.sqrt(v1 * q1 + v2 * q2 + 1.0) + jnp.sqrt(base)
    return d1 * f1 + d2 * f2 + numer / denom


ROWS = 32
BLOCKS = [(r, l) for l in range(0, 256, 128) for r in range(0, 64, ROWS)]


def bit(value, place):
    return lax.rem(lax.div(value, 1 << place), 2)


def tofloat(value):
    return value.astype(F32)


def mid_kernel(grp, node_ref, owner_ref, x_ref, t1_ref, t3_ref, off_ref, off3_ref, z_ref,
               tab1, tab2, tabm, tab3i, tab3o, tab4i, doff, t1s, xh, xl, y1, y2, wmat, x3, v4):
    flat = lax.axis_index("grp") * lax.axis_size("dev") + lax.axis_index("dev")
    h = lax.div(flat, 16)
    ry = lax.rem(flat, 16)
    hf = tofloat(h)
    ryf = tofloat(ry)

    onehot = node_onehot(node_ref)
    for axis in range(2):
        doff[axis] = sum(dot(onehot, off3_ref[p, axis], TN_DIMS) for p in (2, 1, 0))
    for c in range(4):
        t1s[:, c * 64:(c + 1) * 64] = dot(t1_ref[:, c * 64:(c + 1) * 64], onehot).astype(BF16)

    lane = [fiota((1, 128), 1) + k for k in (0, 128)]
    bx = [tofloat(lax.rem(v, 64)) for v in lane]
    by = [4.0 * ryf + tofloat(lax.div(v, 64)) for v in lane]

    def save(tab, index, cycles, rows, lanes):
        cs, sn = trig(cycles)
        tab[index, 0, rows, lanes] = cs
        tab[index, 1, rows, lanes] = sn

    def level1(i, carry):
        c = lax.rem(i, 4)
        u2 = lax.rem(lax.div(i, 4), 4)
        u1 = lax.div(i, 16)
        a1 = (2.0 * hf + tofloat(bit(u1, 0)) + 0.5) / 32.0
        a2 = (tofloat(bit(u1, 1)) + 0.5) / 32.0
        v1, v2 = speeds(jnp.full((1, 128), a1, F32), jnp.full((1, 128), a2, F32))
        sx = 16.0 * (tofloat(bit(c, 0)) - 0.5)
        sy = 16.0 * (tofloat(bit(c, 1)) - 0.5)
        for r, l in BLOCKS:
            rows = slice(r, r + ROWS)
            k = l // 128
            g1 = 32.0 * (2.0 * bx[k] + tofloat(bit(u2, 0)) + 0.5) - HALF
            g2 = 32.0 * (2.0 * by[k] + tofloat(bit(u2, 1)) + 0.5) - HALF
            cycles = freq_cycles(sx + 16.0 * doff[0, rows], sy + 16.0 * doff[1, rows],
                                 g1, g2, a1, a2, v1, v2)
            save(tab1, i, -cycles, rows, slice(l, l + 128))
        return carry

    lax.fori_loop(0, 64, level1, 0)

    def level2(i, carry):
        u2 = lax.rem(i, 4)
        c = lax.rem(lax.div(i, 4), 4)
        u1 = lax.div(i, 16)
        a1 = (2.0 * hf + tofloat(bit(u1, 0)) + 0.5) / 32.0
        a2 = (tofloat(bit(u1, 1)) + 0.5) / 32.0
        v1, v2 = speeds(jnp.full((1, 128), a1, F32), jnp.full((1, 128), a2, F32))
        b1 = (4.0 * hf + 2.0 * tofloat(bit(u1, 0)) + tofloat(bit(u2, 0)) + 0.5) / 64.0
        b2 = (2.0 * tofloat(bit(u1, 1)) + tofloat(bit(u2, 1)) + 0.5) / 64.0
        w1, w2 = speeds(jnp.full((1, 128), b1, F32), jnp.full((1, 128), b2, F32))
        cx = tofloat(bit(c, 0))
        cy = tofloat(bit(c, 1))
        index = (u1 * 4 + u2) * 4 + c
        for r, l in BLOCKS:
            rows = slice(r, r + ROWS)
            k = l // 128
            d1 = 32.0 * off_ref[0, rows]
            d2 = 32.0 * off_ref[1, rows]
            out = freq_cycles(d1, d2, 32.0 * (2.0 * bx[k] + cx + 0.5) - HALF,
                              32.0 * (2.0 * by[k] + cy + 0.5) - HALF, a1, a2, v1, v2)
            inn = freq_cycles(d1 + 32.0 * (cx - 0.5), d2 + 32.0 * (cy - 0.5),
                              64.0 * (bx[k] + 0.5) - HALF, 64.0 * (by[k] + 0.5) - HALF,
                              b1, b2, w1, w2)
            save(tab2, index, out - inn, rows, slice(l, l + 128))
        return carry

    lax.fori_loop(0, 64, level2, 0)

    def middle(u, carry):
        u1 = lax.rem(u, 4)
        u2 = lax.div(u, 4)
        b1 = (4.0 * hf + 2.0 * tofloat(bit(u1, 0)) + tofloat(bit(u2, 0)) + 0.5) / 64.0
        b2 = (2.0 * tofloat(bit(u1, 1)) + tofloat(bit(u2, 1)) + 0.5) / 64.0
        w1, w2 = speeds(jnp.full((1, 128), b1, F32), jnp.full((1, 128), b2, F32))
        for r, l in BLOCKS:
            rows = slice(r, r + ROWS)
            k = l // 128
            out = freq_cycles(64.0 * off_ref[0, rows], 64.0 * off_ref[1, rows],
                              64.0 * (bx[k] + 0.5) - HALF, 64.0 * (by[k] + 0.5) - HALF,
                              b1, b2, w1, w2)
            save(tabm, u, out, rows, slice(l, l + 128))
        return carry

    lax.fori_loop(0, 16, middle, 0)

    n = fiota((1, 128), 1)
    nrow = fiota((128, 16), 0)
    slot = 2 * lax.div(nrow, 16) + lax.rem(nrow, 2)
    owner = (owner_ref[0:1, :] == slot).astype(F32).astype(BF16)
    numbers = fiota((8, 16), 1).astype(F32).astype(BF16)
    column = dot(numbers, owner, NT_DIMS)[0:1, :]
    erow = fiota((256, 16), 0)
    picks = (lax.rem(lax.div(erow, 4), 16) == fiota((256, 16), 1)).astype(F32).astype(BF16)
    wcol = dot(picks, owner, NT_DIMS)
    wlane = fiota((256, 128), 0)
    digit = lax.rem(lax.div(wlane, 2), 2) + 2 * lax.div(wlane, 128)
    wu = lax.rem(lax.div(fiota((256, 128), 1), 2), 8)
    for v2d in range(4):
        keep = jnp.where(digit == v2d, wcol, 0.0)

        def fill(u8, carry):
            wmat[pl.ds(u8 * 256, 256), v2d * 128:(v2d + 1) * 128] = jnp.where(
                wu == u8, keep, 0.0).astype(BF16)
            return carry

        lax.fori_loop(0, 8, fill, 0)

    u8 = lax.rem(lax.div(n, 2), 8)

    def parent(half):
        u = u8 + 8 * half
        u1 = lax.rem(u, 4)
        u2 = lax.div(u, 4)
        return (4.0 * hf + tofloat(2 * lax.rem(u1, 2) + lax.rem(u2, 2)),
                tofloat(2 * lax.div(u1, 2) + lax.div(u2, 2)))

    def level3(half, carry):
        mx, my = parent(half)
        p1 = (mx + 0.5) / 64.0
        p2 = (my + 0.5) / 64.0
        w1, w2 = speeds(p1, p2)
        for r in range(0, 64, ROWS):
            rows = slice(r, r + ROWS)
            d1 = off_ref[0, rows] / 64.0
            d2 = off_ref[1, rows] / 64.0
            s1, s2 = speeds(p1 + d1, p2 + d2)
            for v in range(4):
                f1 = 128.0 * (2.0 * column + (v % 2) + 0.5) - HALF
                f2 = 128.0 * (2.0 * ryf + (v // 2) + 0.5) - HALF
                cycles = space_cycles(d1, d2, p1, p2, s1, s2, w1, w2, f1, f2)
                save(tab3i, half * 4 + v, -cycles, rows, slice(0, 128))
        return carry

    lax.fori_loop(0, 2, level3, 0)

    def level4(i, carry):
        half = lax.div(i, 4)
        jx = tofloat(bit(lax.rem(i, 4), 0))
        jy = tofloat(bit(lax.rem(i, 4), 1))
        mx, my = parent(half)
        p1 = (mx + 0.5) / 64.0
        p2 = (my + 0.5) / 64.0
        w1, w2 = speeds(p1, p2)
        c1 = (2.0 * mx + jx + 0.5) / 128.0
        c2 = (2.0 * my + jy + 0.5) / 128.0
        z1, z2 = speeds(c1, c2)
        for r in range(0, 64, ROWS):
            rows = slice(r, r + ROWS)
            d1 = off_ref[0, rows] / 128.0
            d2 = off_ref[1, rows] / 128.0
            s1, s2 = speeds(c1 + d1, c2 + d2)
            e1 = d1 + (jx - 0.5) / 128.0
            e2 = d2 + (jy - 0.5) / 128.0
            for v in range(4):
                f1 = 128.0 * (2.0 * column + (v % 2) + 0.5) - HALF
                f2 = 128.0 * (2.0 * ryf + (v // 2) + 0.5) - HALF
                cycles = space_cycles(e1, e2, p1, p2, s1, s2, w1, w2, f1, f2)
                save(tab3o, i * 4 + v, cycles, rows, slice(0, 128))
            f1 = 256.0 * (column + 0.5) - HALF
            f2 = 256.0 * (ryf + 0.5) - HALF
            cycles = space_cycles(d1, d2, c1, c2, s1, s2, z1, z2, f1, f2)
            save(tab4i, i, -cycles, rows, slice(0, 128))
        return carry

    lax.fori_loop(0, 8, level4, 0)

    def turn(re, im, tab, index, rows, lanes):
        cs = tab[index, 0, rows, lanes]
        sn = tab[index, 1, rows, lanes]
        return re * cs - im * sn, re * sn + im * cs

    def turned(source, tab, base):
        for c in range(4):
            for r, l in BLOCKS:
                rows = slice(r, r + ROWS)
                re, im = source(c, rows, l)
                parts = turn(re, im, tab, base + c, rows, slice(l, l + 128))
                for p in range(2):
                    hi, lo = split(parts[p])
                    at = slice(c * 64 + r, c * 64 + r + ROWS)
                    to = slice(p * 256 + l, p * 256 + l + 128)
                    xh[at, to] = hi
                    xl[at, to] = lo

    def mixed(table):
        first = dot(table[...], xh[...])
        return first[:64] + first[64:] + dot(table[0:64], xl[...])

    def run1(i, carry):
        u2 = lax.rem(i, 4)
        u1 = lax.div(i, 4)

        def source(c, rows, l):
            lanes = slice(l, l + 128)
            return x_ref[u2 * 4 + c, 0, rows, lanes], x_ref[u2 * 4 + c, 1, rows, lanes]

        turned(source, tab1, (u1 * 4 + u2) * 4)
        y1[u1 * 4 + u2] = mixed(t1s)
        return carry

    lax.fori_loop(0, 16, run1, 0)

    def run2(i, carry):
        u = i
        u1 = lax.rem(u, 4)
        u2 = lax.div(u, 4)

        def source(c, rows, l):
            return (y1[u1 * 4 + c, rows, l:l + 128], y1[u1 * 4 + c, rows, 256 + l:384 + l])

        turned(source, tab2, (u1 * 4 + u2) * 4)
        out = mixed(t1_ref)
        at = pl.multiple_of(lax.rem(u, 8) * 256, 256)
        half = lax.div(u, 8)
        for r, l in BLOCKS:
            rows = slice(r, r + ROWS)
            parts = turn(out[rows, l:l + 128], out[rows, 256 + l:384 + l], tabm, u, rows,
                         slice(l, l + 128))
            for p in range(2):
                hi, lo = split(parts[p])
                y2[half, p * 64 + r:p * 64 + r + ROWS, pl.ds(at + l, 128)] = hi
                y2[half, 128 + p * 64 + r:128 + p * 64 + r + ROWS, pl.ds(at + l, 128)] = lo
        return carry

    lax.fori_loop(0, 16, run2, 0)

    def run3(half, carry):
        both = dot(y2[half], wmat[...])
        summed = both[:128] + both[128:]
        for v in range(4):
            for r in range(0, 64, ROWS):
                rows = slice(r, r + ROWS)
                l = v * 128
                parts = turn(summed[r:r + ROWS, l:l + 128],
                             summed[64 + r:64 + r + ROWS, l:l + 128], tab3i, half * 4 + v, rows,
                             slice(0, 128))
                for p in range(2):
                    hi, lo = split(parts[p])
                    to = slice((v * 2 + p) * 128, (v * 2 + p + 1) * 128)
                    x3[r:r + ROWS, to] = hi
                    x3[64 + r:64 + r + ROWS, to] = lo
                    x3[128 + r:128 + r + ROWS, to] = hi
        for j in range(4):
            out = dot(t3_ref[j * 64:(j + 1) * 64], x3[...])
            for r in range(0, 64, ROWS):
                rows = slice(r, r + ROWS)
                re = None
                for v in range(4):
                    l = v * 256
                    a, b = turn(out[rows, l:l + 128], out[rows, l + 128:l + 256], tab3o,
                                (half * 4 + j) * 4 + v, rows, slice(0, 128))
                    re = a if re is None else re + a
                    im = b if v == 0 else im + b
                re, im = turn(re, im, tab4i, half * 4 + j, rows, slice(0, 128))
                v4[r:r + ROWS] = re
                v4[64 + r:64 + r + ROWS] = im
            flipped = v4[...].T
            for k in range(8):
                z_ref[k, j, pl.ds(pl.multiple_of(half * 16, 16), 16), :] = flipped[k * 16:(k + 1) * 16]
        return carry

    lax.fori_loop(0, 2, run3, 0)


def last_kernel(node_ref, owner_ref, y_ref, tf_ref, off3_ref, o_ref, doff, tmat, yy):
    flat = lax.axis_index("grp") * lax.axis_size("dev") + lax.axis_index("dev")
    own = lax.rem(flat, 16)
    group = lax.div(flat, 16)
    v1 = lax.rem(own, 4)
    v2 = lax.div(own, 4)
    onehot = node_onehot(node_ref)
    for axis in range(2):
        doff[axis] = sum(dot(onehot, off3_ref[p, axis], TN_DIMS) for p in (2, 1, 0))
    zero = jnp.zeros((64, 64), BF16)
    at = pl.multiple_of(v2 * 64, 64)
    parts = [dot(onehot, tf_ref[p, pl.ds(at, 64), :], TN_DIMS).astype(BF16) for p in range(2)]
    for p in range(2):
        for q in range(2):
            for part in range(2):
                for src in range(2):
                    lanes = slice(src * 128 + q * 64, src * 128 + q * 64 + 64)
                    rows = slice(part * 128 + p * 64, part * 128 + p * 64 + 64)
                    use = p == q and not (part == 1 and src == 1)
                    tmat[rows, lanes] = parts[part] if use else zero
    slot_row = 2 * group + fiota((128, 16), 0) // 64 * 0
    ids = fiota((512, 16), 0)
    slot = 2 * group + lax.rem(lax.div(ids, 16), 2)
    owner = (owner_ref[0:1, :] == slot).astype(F32).astype(BF16)
    numbers = fiota((8, 16), 1).astype(F32).astype(BF16)
    column = dot(numbers, owner, NT_DIMS)[0:1, :]
    jx, jy = tofloat(lax.rem(v2, 2)), tofloat(lax.div(v2, 2))
    vx, vy = tofloat(lax.rem(v1, 2)), tofloat(lax.div(v1, 2))

    def run(h, carry):
        for part in range(16):
            block = y_ref[h * 16 + part]
            hi, lo = split(block)
            del hi, lo
            yy[pl.ds(part, 32, stride=16), :] = block
        hi, lo = split(yy[...])
        both = jnp.concatenate([hi, lo], axis=1)
        out = dot(tmat[...], both, NT_DIMS)
        out = out[:128] + out[128:]
        for l in range(0, 512, 128):
            n = fiota((1, 128), 1) + l
            u = lax.div(n, 32)
            u1 = lax.rem(u, 4)
            u2 = lax.div(u, 4)
            mx = 4.0 * tofloat(h) + tofloat(2 * lax.rem(u1, 2) + lax.rem(u2, 2))
            my = tofloat(2 * lax.div(u1, 2) + lax.div(u2, 2))
            c1 = (2.0 * mx + vx + 0.5) / 128.0
            c2 = (2.0 * my + vy + 0.5) / 128.0
            w1, w2 = speeds(c1, c2)
            f1 = 256.0 * (column[:, l:l + 128] + 0.5) - HALF
            f2 = 256.0 * (tofloat(lax.rem(n, 16)) + 0.5) - HALF
            for r in range(0, 64, ROWS):
                d1 = doff[0, r:r + ROWS] / 256.0 + (jx - 0.5) / 256.0
                d2 = doff[1, r:r + ROWS] / 256.0 + (jy - 0.5) / 256.0
                s1, s2 = speeds(c1 + d1, c2 + d2)
                cs, sn = trig(space_cycles(d1, d2, c1, c2, s1, s2, w1, w2, f1, f2))
                re = out[r:r + ROWS, l:l + 128]
                im = out[64 + r:64 + r + ROWS, l:l + 128]
                lanes = pl.ds(pl.multiple_of(h * 512 + l, 128), 128)
                o_ref[0, r:r + ROWS, lanes] = re * cs - im * sn
                o_ref[1, r:r + ROWS, lanes] = re * sn + im * cs
        return carry

    lax.fori_loop(0, 8, run, 0)


VMEM_LIMIT = 60 * 1024 * 1024


def body(weights, owner_map, node_index):
    t1, t3, tf, off, off3 = constants()
    owner = owner_map.reshape(1, 16)
    groups = [list(range(g * 16, g * 16 + 16)) for g in range(lax.axis_size("dev") // 16)]
    x = lax.all_to_all(weights.reshape(2, 64, 16, 256), "dev", 2, 0, axis_index_groups=groups)
    vmem = pl.BlockSpec(memory_space=pltpu.VMEM)
    z = pl.pallas_call(
        functools.partial(mid_kernel, 0),
        out_shape=jax.ShapeDtypeStruct((8, 4, 32, 128), F32),
        in_specs=[vmem] * 7,
        out_specs=vmem,
        scratch_shapes=[
            pltpu.VMEM((64, 2, 64, 256), F32),
            pltpu.VMEM((64, 2, 64, 256), F32),
            pltpu.VMEM((16, 2, 64, 256), F32),
            pltpu.VMEM((8, 2, 64, 128), F32),
            pltpu.VMEM((32, 2, 64, 128), F32),
            pltpu.VMEM((8, 2, 64, 128), F32),
            pltpu.VMEM((2, 64, 128), F32),
            pltpu.VMEM((128, 256), BF16),
            pltpu.VMEM((256, 512), BF16),
            pltpu.VMEM((256, 512), BF16),
            pltpu.VMEM((16, 64, 512), F32),
            pltpu.VMEM((2, 256, 2048), BF16),
            pltpu.VMEM((2048, 512), BF16),
            pltpu.VMEM((192, 1024), BF16),
            pltpu.VMEM((128, 128), F32),
        ],
        compiler_params=pltpu.CompilerParams(vmem_limit_bytes=VMEM_LIMIT),
        name="mid",
    )(node_index, owner, x, t1, t3, off, off3)
    z = jnp.broadcast_to(z[:, None], (8, 4, 4, 32, 128)).reshape(128, 32, 128)
    y = lax.all_to_all(z, ("grp", "dev"), 0, 0, tiled=True)
    return pl.pallas_call(
        last_kernel,
        out_shape=jax.ShapeDtypeStruct((2, 64, 4096), F32),
        in_specs=[vmem] * 5,
        out_specs=vmem,
        scratch_shapes=[
            pltpu.VMEM((2, 64, 128), F32),
            pltpu.VMEM((256, 256), BF16),
            pltpu.VMEM((512, 128), F32),
        ],
        compiler_params=pltpu.CompilerParams(vmem_limit_bytes=VMEM_LIMIT),
        name="last",
    )(node_index, owner, y, tf, off3)


def solution(mesh):
    in_specs = (P(None, None, ("grp", "dev")), P(), P())
    out_specs = P(None, None, ("grp", "dev"))
    return jax.shard_map(body, mesh=mesh, in_specs=in_specs, out_specs=out_specs, check_vma=False)
```

time: 580 us -> 134 us (0.23); the launches traced: 571 us -> 134 us
  waiting for transfers between devices: 236 us -> 0 us
  other arithmetic: 156 us -> 0 us
  between operations: 72 us -> 0.02 us
  Pallas kernels: 0 us -> 56.9 us
  blocking collectives: 42.1 us -> 72.4 us
  local copies, waits for them, and re-layouts: 33.8 us -> 4.77 us
  matrix products: 20.4 us -> 0 us
  starting transfers between devices: 11.4 us -> 0 us
    ppermute x10 -> x0, waiting for transfers between devices: 236 us -> none  [from_partner(): lax.ppermute(array, axis, [(i, i ^ 1 << bit) for i in range(lax.axis_size...]
    sub x26 -> x0, other arithmetic: 122 us -> none  [the longest x14 116 us: rotate(): values[0] * cosine - values[1] * sine_part]
    pallas_call x0 -> x2, Pallas kernels: none -> 56.9 us  [the longest x1 47.4 us: body(): pl.pallas_call(functools.partial(mid_kernel, 0), out_shape=jax.ShapeDtype...]
    all_to_all x1 -> x2, blocking collectives: 42.1 us -> 72.4 us  [the longest x1 38.2 us: body(): y = lax.all_to_all(z, ('grp', 'dev'), 0, 0, tiled=True)]
    dot_general x10 -> x0, matrix products: 20.4 us -> none  [the longest x8 16.4 us: freq_level(): jnp.einsum('ts,rsn->rtn', table_now, rotate(values, -phase_angle), precis...]
    ppermute x10 -> x0, starting transfers between devices: 11.4 us -> none  [from_partner(): lax.ppermute(array, axis, [(i, i ^ 1 << bit) for i in range(lax.axis_size...]
    div x29 -> x0, other arithmetic: 7.63 us -> none  [lagrange(): product * (places - points[other_id])]
    all_to_all x1 -> x0, other arithmetic: 7.31 us -> none  [finish_levels(): lax.all_to_all(blocks.reshape(2, node_count, devices, per_source), ('grp'...]
  transfers between devices with their start and end apart: 10 -> 0, of which waited for: 7 -> 0; matrix products, arithmetic and copies ran while one was open for 11% -> 0% of each run, Pallas kernels for 0% -> 0%
where the time goes in v1:
time: 134 us
  blocking collectives  72.4 us (54%)
  Pallas kernels  56.9 us (42%)
  local copies, waits for them, and re-layouts  4.77 us (4%)
    pallas_call x1, Pallas kernels, body(): pl.pallas_call(functools.partial(mid_kernel, 0), out_shape=jax.ShapeDtype...  47.4 us
    all_to_all x1, blocking collectives, body(): y = lax.all_to_all(z, ('grp', 'dev'), 0, 0, tiled=True)  38.2 us
    all_to_all x1, blocking collectives, body(): lax.all_to_all(weights.reshape(2, 64, 16, 256), 'dev', 2, 0, axis_index_g...  34.2 us
    pallas_call x1, Pallas kernels, body(): pl.pallas_call(last_kernel, out_shape=jax.ShapeDtypeStruct((2, 64, 4096),...  9.45 us

profile of v1, /device:TPU:1, one launch (start us, length us, event | category | flops | bytes accessed | tf_op | source)
XLA Modules:
  0.0 134.0 jit_solution(17602897342386473206)
XLA Ops:
  0.0 2.3 %copy.11 = f32[16,8,16,256]{3,2,1,0:T(8,128)S(1)} copy(f32[16,8,16,256]{3,1,2,0:T(8,128)} %bitcast.14) | data formatting | bytes 4194304
  2.3 1.2 copy.10
  3.5 34.2 %all_to_all.20 = f32[1,2,64,16,256]{4,2,1,0,3:T(8,128)} all-to-all(f32[1,2,64,16,256]{4,2,1,0,3:T(8,128)S(1)} %copy.10), channel_id=1, replica_groups={{0,1,2,3,4,5,6,7,8,9,10,11,12,13,14,15},{16,17,18,19,20,21,22,23,24,25,..., dimensions={3} | all-to-all | bytes 4194304 | tf_op jit(solution)/shard_map/all_to_all | solution.py:489
  37.6 47.4 %mid.1 = f32[8,4,32,128]{3,2,1,0:T(8,128)} custom-call(s32[2,64]{1,0:T(2,128)} %node_ref.3, s32[1,16]{1,0:T(1,128)} %bitcast.15, f32[16,2,64,256]{3,2,1,0:T(8,128)} %bitcast.12, bf16[128,256]{1,0:T(8,128)(2,1)} %constant.10.clone.t1_ref, bf16[256,192]{1,0:T(8,128)(2,1)} %constant.11.clone.t3_ref, f32[2,64,128]{2,1,0:T(8,128)} %constant.12.clone.off_ref, ...), custom_call_target="tpu_custom_call" | custom-call | tf_op jit(solution)/shard_map/mid/pallas_call | solution.py:491
  85.0 1.3 broadcast_in_dim.2
  86.3 38.2 %all_to_all.21.y_ref = f32[128,32,128]{2,1,0:T(8,128)} all-to-all(f32[128,32,128]{2,1,0:T(8,128)S(1)} %bitcast.11), channel_id=1, replica_groups=mesh['grp'=2,'dev'=64] {'grp','dev'}, dimensions={0} | all-to-all | bytes 4194304 | tf_op jit(solution)/shard_map/all_to_all | solution.py:517
  124.5 9.5 %last.1 = f32[2,64,4096]{2,1,0:T(8,128)} custom-call(s32[2,64]{1,0:T(2,128)} %node_ref.3, s32[1,16]{1,0:T(1,128)} %bitcast.16, f32[128,32,128]{2,1,0:T(8,128)} %all_to_all.21.y_ref, bf16[2,256,64]{2,1,0:T(8,128)(2,1)} %constant.14.clone.tf_ref, bf16[3,2,64,128]{3,2,1,0:T(8,128)(2,1)} %constant.13.clone.off3_ref), custom_call_target="tpu_custom_call" | custom-call | tf_op jit(solution)/shard_map/last/pallas_call | solution.py:518

commit v2 on v1

v2 whole, which is shorter than its diff:
```python
import functools
import math

import jax
import jax.numpy as jnp
import numpy as np
from jax import lax
from jax.experimental import pallas as pl
from jax.experimental.pallas import tpu as pltpu
from jax.sharding import PartitionSpec as P

F32 = jnp.float32
BF16 = jnp.bfloat16
HALF = 2048.0
NT_DIMS = (((1,), (1,)), ((), ()))
TN_DIMS = (((0,), (0,)), ((), ()))
NN_DIMS = (((1,), (0,)), ((), ()))


def fit(function, count):
    angle = (np.arange(64) + 0.5) * np.pi / 64
    points = 0.125 + 0.125 * np.cos(angle)
    cheb = np.polynomial.chebyshev.Chebyshev.fit(
        points, function(np.sqrt(points)), count - 1, domain=[0.0, 0.25]
    )
    return [float(c) for c in cheb.convert(kind=np.polynomial.Polynomial).coef]


ROOT2 = math.sqrt(2.0)
SIN_COEF = fit(lambda r: ROOT2 * np.sin(np.pi * r) / r, 5)
COS_COEF = fit(lambda r: ROOT2 * np.cos(np.pi * r), 5)


def horner(coef, u):
    total = coef[-1] * u + coef[-2]
    for c in coef[-3::-1]:
        total = total * u + c
    return total


def trig(cycles):
    r = cycles - jnp.round(cycles)
    u = r * r
    s = horner(SIN_COEF, u) * r
    c = horner(COS_COEF, u)
    return 1.0 - s * s, s * c


def cheb_nodes():
    return 0.5 * np.cos(np.pi * (2.0 * np.arange(8) + 1.0) / 16.0)


def canon_tables():
    z = cheb_nodes()
    basis = np.zeros((2, 8, 8))
    for c in range(2):
        places = z / 2 + c / 2 - 0.25
        for i in range(8):
            value = np.ones(8)
            for k in range(8):
                if k != i:
                    value = value * (places - z[k]) / (z[i] - z[k])
            basis[c, i] = value
    return [np.kron(basis[c % 2], basis[c // 2]) for c in range(4)]


def split_np(a):
    hi = np.asarray(a, np.float32).astype(BF16)
    lo = (np.asarray(a, np.float64) - hi.astype(np.float64)).astype(np.float32).astype(BF16)
    return hi, lo


def constants():
    z = cheb_nodes().astype(np.float32)
    tables = canon_tables()
    t_in = np.concatenate(tables, axis=1)
    t_out = np.concatenate([t.T for t in tables], axis=0)
    in_h, in_l = split_np(t_in)
    out_h, out_l = split_np(t_out)
    t1 = np.concatenate([in_h, in_l], axis=0)
    t3 = np.concatenate([out_h, out_h, out_l], axis=1)
    tf = np.stack([out_h, out_l])
    ox = np.repeat(z, 8)
    oy = np.tile(z, 8)
    off = np.stack([np.broadcast_to(o[:, None], (64, 128)) for o in (ox, oy)])
    pieces = []
    rest = off.astype(np.float32)
    for _ in range(3):
        piece = rest.astype(BF16)
        pieces.append(piece)
        rest = rest - piece.astype(np.float32)
    return t1, t3, tf, np.ascontiguousarray(off, np.float32), np.stack(pieces)


def fiota(shape, axis):
    return lax.broadcasted_iota(jnp.int32, shape, axis)


def node_onehot(node_ref):
    flat = node_ref[0:1, :] * 8 + node_ref[1:2, :]
    return (fiota((64, 64), 0) == flat).astype(F32).astype(BF16)


def dot(a, b, dims=NN_DIMS):
    return lax.dot_general(a, b, dims, preferred_element_type=F32)


def split(x):
    hi = x.astype(BF16)
    return hi, (x - hi.astype(F32)).astype(BF16)


def from_sines(s1, c1, s2, c2):
    one = (2.0 + s1 * s2) * 0.0625
    two = (2.0 + c1 * c2) * 0.0625
    return one * one, two * two


def speeds(x1, x2):
    c1, s1 = trig(x1)
    c2, s2 = trig(x2)
    return from_sines(s1, c1, s2, c2)


def speeds_sum(row, col):
    sines = []
    for (ca, sa), (cb, sb) in zip(row, col):
        sines += [sa * cb + ca * sb, ca * cb - sa * sb]
    return from_sines(*sines)


def root(x):
    return x * lax.rsqrt(x)


def freq_columns(d1, d2, a1, a2, v1, v2):
    e1 = v1 * d1
    e2 = v2 * d2
    return 2.0 * e1, 2.0 * e2, e1 * d1 + e2 * d2, a1 * d1 + a2 * d2


def freq_row(g1, g2, v1, v2):
    square = v1 * g1 * g1 + v2 * g2 * g2 + 1.0
    return g1, g2, square, root(square)


def freq_cycles(columns, row):
    e1, e2, e0, linear = columns
    g1, g2, square, base = row
    numer = e1 * g1 + e2 * g2 + e0
    return linear + numer / (root(square + numer) + base)


def space_cycles(d1, d2, v1, v2, w1, w2, f1, f2):
    q1 = f1 * f1
    q2 = f2 * f2
    base = w1 * q1 + w2 * q2 + 1.0
    numer = (v1 - w1) * q1 + (v2 - w2) * q2
    return d1 * f1 + d2 * f2 + numer / (root(base + numer) + root(base))


ROWS = 32
BLOCKS = [(r, l) for l in range(0, 256, 128) for r in range(0, 64, ROWS)]
MESH = pl.DeviceIdType.MESH


def bit(value, place):
    return lax.rem(lax.div(value, 1 << place), 2)


def tofloat(value):
    return value.astype(F32)


def splat(value):
    return jnp.full((1, 128), value, F32)


def save(tab, index, cycles, rows, lanes):
    cs, sn = trig(cycles)
    tab[index, 0, rows, lanes] = cs
    tab[index, 1, rows, lanes] = sn


def turn(re, im, tab, index, rows, lanes):
    cs = tab[index, 0, rows, lanes]
    sn = tab[index, 1, rows, lanes]
    return re * cs - im * sn, re * sn + im * cs


def columns_of(owner_ref, slot):
    owner = (owner_ref[0:1, :] == slot).astype(F32).astype(BF16)
    numbers = fiota((8, 16), 1).astype(F32).astype(BF16)
    return dot(numbers, owner, NT_DIMS)[0:1, :], owner


def kernel(n_dev, n_all, node_ref, owner_ref, w_hbm, t1_hbm, t3_hbm, tf_hbm, off_hbm, off3_hbm,
           o_ref, x_ref, t1_ref, t3_ref, tf_ref, off_ref, off3_ref, z_ref, y_ref, tab1, tab2,
           tabm, tab3i, tab3o, tab4i, tabf, part, doff, t1s, xh, xl, y1, y2, wmat, x3, v4, tmat,
           yy, send1, recv1, send2, recv2, local):
    flat = lax.axis_index("grp") * n_dev + lax.axis_index("dev")
    h = lax.div(flat, 16)
    ry = lax.rem(flat, 16)
    hf = tofloat(h)
    ryf = tofloat(ry)

    def place(device):
        return lax.div(device, n_dev), lax.rem(device, n_dev)

    barrier = pltpu.get_barrier_semaphore()

    def greet(i, carry):
        pl.semaphore_signal(barrier, inc=1, device_id=place(lax.rem(flat + i, n_all)),
                            device_id_type=MESH)
        return carry

    lax.fori_loop(1, n_all, greet, 0)
    pl.semaphore_wait(barrier, n_all - 1)

    def chunk(m):
        return w_hbm.at[:, :, pl.ds(pl.multiple_of(m * 256, 256), 256)]

    def exchange1(i):
        m = lax.rem(ry + i, 16)
        return pltpu.make_async_remote_copy(
            src_ref=chunk(m), dst_ref=x_ref.at[ry], send_sem=send1.at[i], recv_sem=recv1.at[i],
            device_id=place(h * 16 + m), device_id_type=MESH)

    for i in range(1, 16):
        exchange1(i).start()
    own1 = pltpu.make_async_copy(chunk(ry), x_ref.at[ry], recv1.at[0])
    own1.start()
    loads = [pltpu.make_async_copy(a, b, local.at[i]) for i, (a, b) in enumerate(
        [(t1_hbm, t1_ref), (t3_hbm, t3_ref), (tf_hbm, tf_ref), (off_hbm, off_ref),
         (off3_hbm, off3_ref)])]
    for load in loads:
        load.start()
    for load in loads:
        load.wait()

    onehot = node_onehot(node_ref)
    for axis in range(2):
        doff[axis] = sum(dot(onehot, off3_ref[p, axis], TN_DIMS) for p in (2, 1, 0))
    for c in range(4):
        t1s[:, c * 64:(c + 1) * 64] = dot(t1_ref[:, c * 64:(c + 1) * 64], onehot).astype(BF16)

    lane = [fiota((1, 128), 1) + k for k in (0, 128)]
    bx = [tofloat(lax.rem(v, 64)) for v in lane]
    by = [4.0 * ryf + tofloat(lax.div(v, 64)) for v in lane]

    def level1(i, carry):
        c = lax.rem(i, 4)
        u1 = lax.div(i, 4)
        a1 = (2.0 * hf + tofloat(bit(u1, 0)) + 0.5) / 32.0
        a2 = (tofloat(bit(u1, 1)) + 0.5) / 32.0
        v1, v2 = speeds(splat(a1), splat(a2))
        sx = 16.0 * (tofloat(bit(c, 0)) - 0.5)
        sy = 16.0 * (tofloat(bit(c, 1)) - 0.5)
        cols = [freq_columns(sx + 16.0 * doff[0, r:r + ROWS], sy + 16.0 * doff[1, r:r + ROWS],
                             -a1, -a2, v1, v2) for r in range(0, 64, ROWS)]

        def inner(u2, carry):
            for l in range(0, 256, 128):
                k = l // 128
                row = freq_row(32.0 * (2.0 * bx[k] + tofloat(bit(u2, 0)) + 0.5) - HALF,
                               32.0 * (2.0 * by[k] + tofloat(bit(u2, 1)) + 0.5) - HALF, v1, v2)
                g1, g2, square, base = row
                for r in range(0, 64, ROWS):
                    e1, e2, e0, linear = cols[r // ROWS]
                    numer = e1 * g1 + e2 * g2 + e0
                    cycles = linear - numer / (root(square + numer) + base)
                    save(tab1, i * 4 + u2, cycles, slice(r, r + ROWS), slice(l, l + 128))
            return carry

        lax.fori_loop(0, 4, inner, 0)
        return carry

    lax.fori_loop(0, 16, level1, 0)

    def level2(i, carry):
        c = lax.rem(i, 4)
        u1 = lax.div(i, 4)
        a1 = (2.0 * hf + tofloat(bit(u1, 0)) + 0.5) / 32.0
        a2 = (tofloat(bit(u1, 1)) + 0.5) / 32.0
        v1, v2 = speeds(splat(a1), splat(a2))
        cx = tofloat(bit(c, 0))
        cy = tofloat(bit(c, 1))
        for l in range(0, 256, 128):
            k = l // 128
            row = freq_row(32.0 * (2.0 * bx[k] + cx + 0.5) - HALF,
                           32.0 * (2.0 * by[k] + cy + 0.5) - HALF, v1, v2)
            for r in range(0, 64, ROWS):
                cols = freq_columns(32.0 * off_ref[0, r:r + ROWS], 32.0 * off_ref[1, r:r + ROWS],
                                    a1, a2, v1, v2)
                part[r:r + ROWS, l:l + 128] = freq_cycles(cols, row)

        def inner(u2, carry):
            b1 = (4.0 * hf + 2.0 * tofloat(bit(u1, 0)) + tofloat(bit(u2, 0)) + 0.5) / 64.0
            b2 = (2.0 * tofloat(bit(u1, 1)) + tofloat(bit(u2, 1)) + 0.5) / 64.0
            w1, w2 = speeds(splat(b1), splat(b2))
            rows = [freq_row(64.0 * (bx[k] + 0.5) - HALF, 64.0 * (by[k] + 0.5) - HALF, w1, w2)
                    for k in range(2)]
            for r in range(0, 64, ROWS):
                cols = freq_columns(32.0 * (off_ref[0, r:r + ROWS] + (cx - 0.5)),
                                    32.0 * (off_ref[1, r:r + ROWS] + (cy - 0.5)), b1, b2, w1, w2)
                for l in range(0, 256, 128):
                    cycles = part[r:r + ROWS, l:l + 128] - freq_cycles(cols, rows[l // 128])
                    save(tab2, i * 4 + u2, cycles, slice(r, r + ROWS), slice(l, l + 128))
            return carry

        lax.fori_loop(0, 4, inner, 0)
        return carry

    lax.fori_loop(0, 16, level2, 0)

    def middle(u, carry):
        u1 = lax.rem(u, 4)
        u2 = lax.div(u, 4)
        b1 = (4.0 * hf + 2.0 * tofloat(bit(u1, 0)) + tofloat(bit(u2, 0)) + 0.5) / 64.0
        b2 = (2.0 * tofloat(bit(u1, 1)) + tofloat(bit(u2, 1)) + 0.5) / 64.0
        w1, w2 = speeds(splat(b1), splat(b2))
        rows = [freq_row(64.0 * (bx[k] + 0.5) - HALF, 64.0 * (by[k] + 0.5) - HALF, w1, w2)
                for k in range(2)]
        for r in range(0, 64, ROWS):
            cols = freq_columns(64.0 * off_ref[0, r:r + ROWS], 64.0 * off_ref[1, r:r + ROWS],
                                b1, b2, w1, w2)
            for l in range(0, 256, 128):
                save(tabm, u, freq_cycles(cols, rows[l // 128]), slice(r, r + ROWS),
                     slice(l, l + 128))
        return carry

    lax.fori_loop(0, 16, middle, 0)

    n = fiota((1, 128), 1)
    nrow = fiota((128, 16), 0)
    column, owner = columns_of(owner_ref, 2 * lax.div(nrow, 16) + lax.rem(nrow, 2))
    erow = fiota((256, 16), 0)
    picks = (lax.rem(lax.div(erow, 4), 16) == fiota((256, 16), 1)).astype(F32).astype(BF16)
    wcol = dot(picks, owner, NT_DIMS)
    wlane = fiota((256, 128), 0)
    digit = lax.rem(lax.div(wlane, 2), 2) + 2 * lax.div(wlane, 128)
    wu = lax.rem(lax.div(fiota((256, 128), 1), 2), 8)
    for v2d in range(4):
        keep = jnp.where(digit == v2d, wcol, 0.0)

        def fill(u8, carry):
            wmat[pl.ds(pl.multiple_of(u8 * 256, 256), 256), v2d * 128:(v2d + 1) * 128] = jnp.where(
                wu == u8, keep, 0.0).astype(BF16)
            return carry

        lax.fori_loop(0, 8, fill, 0)

    u8 = lax.rem(lax.div(n, 2), 8)

    def parent(u):
        u1 = lax.rem(u, 4)
        u2 = lax.div(u, 4)
        return (tofloat(2 * lax.rem(u1, 2) + lax.rem(u2, 2)),
                tofloat(2 * lax.div(u1, 2) + lax.div(u2, 2)))

    def level3(half, carry):
        mx, my = parent(u8 + 8 * half)
        p1 = (4.0 * hf + mx + 0.5) / 64.0
        p2 = (my + 0.5) / 64.0
        row = (trig(p1), trig(p2))
        w1, w2 = from_sines(row[0][1], row[0][0], row[1][1], row[1][0])
        for r in range(0, 64, ROWS):
            rows = slice(r, r + ROWS)
            d1 = off_ref[0, rows] / 64.0
            d2 = off_ref[1, rows] / 64.0
            s1, s2 = speeds_sum(row, (trig(d1), trig(d2)))
            for v in range(4):
                f1 = 128.0 * (2.0 * column + (v % 2) + 0.5) - HALF
                f2 = 128.0 * (2.0 * ryf + (v // 2) + 0.5) - HALF
                cycles = space_cycles(d1, d2, s1, s2, w1, w2, f1, f2)
                save(tab3i, half * 4 + v, -cycles, rows, slice(0, 128))
        return carry

    lax.fori_loop(0, 2, level3, 0)

    def level4(i, carry):
        half = lax.div(i, 4)
        jx = tofloat(bit(lax.rem(i, 4), 0))
        jy = tofloat(bit(lax.rem(i, 4), 1))
        mx, my = parent(u8 + 8 * half)
        mx = 4.0 * hf + mx
        w1, w2 = speeds((mx + 0.5) / 64.0, (my + 0.5) / 64.0)
        c1 = (2.0 * mx + jx + 0.5) / 128.0
        c2 = (2.0 * my + jy + 0.5) / 128.0
        row = (trig(c1), trig(c2))
        z1, z2 = from_sines(row[0][1], row[0][0], row[1][1], row[1][0])
        for r in range(0, 64, ROWS):
            rows = slice(r, r + ROWS)
            d1 = off_ref[0, rows] / 128.0
            d2 = off_ref[1, rows] / 128.0
            s1, s2 = speeds_sum(row, (trig(d1), trig(d2)))
            e1 = d1 + (jx - 0.5) / 128.0
            e2 = d2 + (jy - 0.5) / 128.0
            for v in range(4):
                f1 = 128.0 * (2.0 * column + (v % 2) + 0.5) - HALF
                f2 = 128.0 * (2.0 * ryf + (v // 2) + 0.5) - HALF
                cycles = space_cycles(e1, e2, s1, s2, w1, w2, f1, f2)
                save(tab3o, i * 4 + v, cycles, rows, slice(0, 128))
            f1 = 256.0 * (column + 0.5) - HALF
            f2 = 256.0 * (ryf + 0.5) - HALF
            cycles = space_cycles(d1, d2, s1, s2, z1, z2, f1, f2)
            save(tab4i, i, -cycles, rows, slice(0, 128))
        return carry

    lax.fori_loop(0, 8, level4, 0)

    own1.wait()
    for i in range(1, 16):
        exchange1(i).wait()

    def turned(source, tab, index):
        for c in range(4):
            for r, l in BLOCKS:
                rows = slice(r, r + ROWS)
                re, im = source(c, rows, l)
                parts = turn(re, im, tab, index(c), rows, slice(l, l + 128))
                for p in range(2):
                    hi, lo = split(parts[p])
                    at = slice(c * 64 + r, c * 64 + r + ROWS)
                    to = slice(p * 256 + l, p * 256 + l + 128)
                    xh[at, to] = hi
                    xl[at, to] = lo

    def mixed(table):
        first = dot(table[...], xh[...])
        return first[:64] + first[64:] + dot(table[0:64], xl[...])

    def run1(i, carry):
        u2 = lax.rem(i, 4)
        u1 = lax.div(i, 4)

        def source(c, rows, l):
            lanes = slice(l, l + 128)
            return x_ref[u2 * 4 + c, 0, rows, lanes], x_ref[u2 * 4 + c, 1, rows, lanes]

        turned(source, tab1, lambda c: (u1 * 4 + c) * 4 + u2)
        y1[u1 * 4 + u2] = mixed(t1s)
        return carry

    lax.fori_loop(0, 16, run1, 0)

    def run2(u, carry):
        u1 = lax.rem(u, 4)
        u2 = lax.div(u, 4)

        def source(c, rows, l):
            return (y1[u1 * 4 + c, rows, l:l + 128], y1[u1 * 4 + c, rows, 256 + l:384 + l])

        turned(source, tab2, lambda c: (u1 * 4 + c) * 4 + u2)
        out = mixed(t1_ref)
        at = pl.multiple_of(lax.rem(u, 8) * 256, 256)
        half = lax.div(u, 8)
        for r, l in BLOCKS:
            rows = slice(r, r + ROWS)
            parts = turn(out[rows, l:l + 128], out[rows, 256 + l:384 + l], tabm, u, rows,
                         slice(l, l + 128))
            for p in range(2):
                hi, lo = split(parts[p])
                y2[half, p * 64 + r:p * 64 + r + ROWS, pl.ds(at + l, 128)] = hi
                y2[half, 128 + p * 64 + r:128 + p * 64 + r + ROWS, pl.ds(at + l, 128)] = lo
        return carry

    lax.fori_loop(0, 16, run2, 0)

    def run3(half, carry):
        both = dot(y2[half], wmat[...])
        summed = both[:128] + both[128:]
        for v in range(4):
            for r in range(0, 64, ROWS):
                rows = slice(r, r + ROWS)
                l = v * 128
                parts = turn(summed[r:r + ROWS, l:l + 128],
                             summed[64 + r:64 + r + ROWS, l:l + 128], tab3i, half * 4 + v, rows,
                             slice(0, 128))
                for p in range(2):
                    hi, lo = split(parts[p])
                    to = slice((v * 2 + p) * 128, (v * 2 + p + 1) * 128)
                    x3[r:r + ROWS, to] = hi
                    x3[64 + r:64 + r + ROWS, to] = lo
                    x3[128 + r:128 + r + ROWS, to] = hi
        for j in range(4):
            out = dot(t3_ref[j * 64:(j + 1) * 64], x3[...])
            for r in range(0, 64, ROWS):
                rows = slice(r, r + ROWS)
                re = None
                for v in range(4):
                    l = v * 256
                    a, b = turn(out[rows, l:l + 128], out[rows, l + 128:l + 256], tab3o,
                                (half * 4 + j) * 4 + v, rows, slice(0, 128))
                    re = a if re is None else re + a
                    im = b if v == 0 else im + b
                re, im = turn(re, im, tab4i, half * 4 + j, rows, slice(0, 128))
                v4[r:r + ROWS] = re
                v4[64 + r:64 + r + ROWS] = im
            flipped = v4[...].T
            for k in range(8):
                z_ref[k, j, pl.ds(pl.multiple_of(half * 16, 16), 16), :] = flipped[k * 16:(k + 1) * 16]
        return carry

    lax.fori_loop(0, 2, run3, 0)

    def exchange2(i):
        to = lax.rem(flat + i, n_all)
        return pltpu.make_async_remote_copy(
            src_ref=z_ref.at[lax.div(to, 16), lax.rem(to, 4)], dst_ref=y_ref.at[flat],
            send_sem=send2, recv_sem=recv2.at[h], device_id=place(to), device_id_type=MESH)

    def send(i, carry):
        exchange2(i).start()
        return carry

    lax.fori_loop(1, n_all, send, 0)
    own2 = pltpu.make_async_copy(z_ref.at[h, lax.rem(flat, 4)], y_ref.at[flat], recv2.at[h])
    own2.start()

    v1d = lax.rem(ry, 4)
    v2d = lax.div(ry, 4)
    zero = jnp.zeros((64, 64), BF16)
    pieces = [dot(onehot, tf_ref[p, pl.ds(pl.multiple_of(v2d * 64, 64), 64), :],
                  TN_DIMS).astype(BF16) for p in range(2)]
    for p in range(2):
        for q in range(2):
            for piece in range(2):
                for low in range(2):
                    lanes = slice(low * 128 + q * 64, low * 128 + q * 64 + 64)
                    rows = slice(piece * 128 + p * 64, piece * 128 + p * 64 + 64)
                    use = p == q and not (piece == 1 and low == 1)
                    tmat[rows, lanes] = pieces[piece] if use else zero
    ids = fiota((512, 16), 0)
    column, _ = columns_of(owner_ref, 2 * h + lax.rem(lax.div(ids, 16), 2))
    jx, jy = tofloat(lax.rem(v2d, 2)), tofloat(lax.div(v2d, 2))
    vx, vy = tofloat(lax.rem(v1d, 2)), tofloat(lax.div(v1d, 2))
    f2 = 256.0 * (tofloat(lax.rem(n, 16)) + 0.5) - HALF

    def level5(src, carry):
        for l in range(0, 512, 128):
            mx, my = parent(lax.div(n + l, 32))
            c1 = (2.0 * (4.0 * tofloat(src) + mx) + vx + 0.5) / 128.0
            c2 = (2.0 * my + vy + 0.5) / 128.0
            row = (trig(c1), trig(c2))
            w1, w2 = from_sines(row[0][1], row[0][0], row[1][1], row[1][0])
            f1 = 256.0 * (column[:, l:l + 128] + 0.5) - HALF
            for r in range(0, 64, ROWS):
                d1 = (doff[0, r:r + ROWS] + (jx - 0.5)) / 256.0
                d2 = (doff[1, r:r + ROWS] + (jy - 0.5)) / 256.0
                s1, s2 = speeds_sum(row, (trig(d1), trig(d2)))
                save(tabf, src, space_cycles(d1, d2, s1, s2, w1, w2, f1, f2),
                     slice(r, r + ROWS), slice(l, l + 128))
        return carry

    lax.fori_loop(0, 8, level5, 0)

    def run4(src, carry):
        landed = y_ref.at[pl.ds(pl.multiple_of(src * 16, 16), 16)]
        pltpu.make_async_copy(landed, landed, recv2.at[src]).wait()
        for m in range(16):
            yy[pl.ds(m, 32, stride=16), :] = y_ref[src * 16 + m]
        hi, lo = split(yy[...])
        out = dot(tmat[...], jnp.concatenate([hi, lo], axis=1), NT_DIMS)
        out = out[:128] + out[128:]
        for l in range(0, 512, 128):
            lanes = pl.ds(pl.multiple_of(src * 512 + l, 128), 128)
            for r in range(0, 64, ROWS):
                rows = slice(r, r + ROWS)
                re, im = turn(out[r:r + ROWS, l:l + 128], out[64 + r:64 + r + ROWS, l:l + 128],
                              tabf, src, rows, slice(l, l + 128))
                o_ref[0, rows, lanes] = re
                o_ref[1, rows, lanes] = im
        return carry

    lax.fori_loop(0, 8, run4, 0)
    sent = y_ref.at[pl.ds(0, n_all - 1)]
    pltpu.make_async_copy(sent, sent, send2).wait()


VMEM_LIMIT = 62 * 1024 * 1024


def body(weights, owner_map, node_index):
    t1, t3, tf, off, off3 = constants()
    n_dev = lax.axis_size("dev")
    n_all = lax.axis_size("grp") * n_dev
    vmem = pl.BlockSpec(memory_space=pltpu.VMEM)
    hbm = pl.BlockSpec(memory_space=pl.ANY)
    dma = pltpu.SemaphoreType.DMA
    return pl.pallas_call(
        functools.partial(kernel, n_dev, n_all),
        out_shape=jax.ShapeDtypeStruct((2, 64, 4096), F32),
        in_specs=[vmem] * 2 + [hbm] * 6,
        out_specs=vmem,
        scratch_shapes=[
            pltpu.VMEM((16, 2, 64, 256), F32),
            pltpu.VMEM(t1.shape, BF16),
            pltpu.VMEM(t3.shape, BF16),
            pltpu.VMEM(tf.shape, BF16),
            pltpu.VMEM(off.shape, F32),
            pltpu.VMEM(off3.shape, BF16),
            pltpu.VMEM((8, 4, 32, 128), F32),
            pltpu.VMEM((128, 32, 128), F32),
            pltpu.VMEM((64, 2, 64, 256), F32),
            pltpu.VMEM((64, 2, 64, 256), F32),
            pltpu.VMEM((16, 2, 64, 256), F32),
            pltpu.VMEM((8, 2, 64, 128), F32),
            pltpu.VMEM((32, 2, 64, 128), F32),
            pltpu.VMEM((8, 2, 64, 128), F32),
            pltpu.VMEM((8, 2, 64, 512), F32),
            pltpu.VMEM((64, 256), F32),
            pltpu.VMEM((2, 64, 128), F32),
            pltpu.VMEM((128, 256), BF16),
            pltpu.VMEM((256, 512), BF16),
            pltpu.VMEM((256, 512), BF16),
            pltpu.VMEM((16, 64, 512), F32),
            pltpu.VMEM((2, 256, 2048), BF16),
            pltpu.VMEM((2048, 512), BF16),
            pltpu.VMEM((192, 1024), BF16),
            pltpu.VMEM((128, 128), F32),
            pltpu.VMEM((256, 256), BF16),
            pltpu.VMEM((512, 128), F32),
            dma((16,)),
            dma((16,)),
            dma(()),
            dma((8,)),
            dma((5,)),
        ],
        compiler_params=pltpu.CompilerParams(
            vmem_limit_bytes=VMEM_LIMIT, collective_id=0, has_side_effects=True),
        name="butterfly",
    )(node_index, owner_map.reshape(1, 16), weights, t1, t3, tf, off, off3)


def solution(mesh):
    in_specs = (P(None, None, ("grp", "dev")), P(), P())
    out_specs = P(None, None, ("grp", "dev"))
    return jax.shard_map(body, mesh=mesh, in_specs=in_specs, out_specs=out_specs, check_vma=False)
```

time: 134 us -> 95.7 us (0.71)
  blocking collectives: 72.4 us -> 0 us
  Pallas kernels: 56.9 us -> 92.4 us
  local copies, waits for them, and re-layouts: 4.77 us -> 3.11 us
    all_to_all x2 -> x0, blocking collectives: 72.4 us -> none  [the longest x1 38.2 us: body(): y = lax.all_to_all(z, ('grp', 'dev'), 0, 0, tiled=True)]
    pallas_call x2 -> x1, Pallas kernels: 56.9 us -> 92.4 us  [body(): pl.pallas_call(functools.partial(kernel, n_dev, n_all), out_shape=jax.Sha...]
where the time goes in v2:
time: 95.7 us; the launch traced here: 95.5 us
  Pallas kernels  92.4 us (97%)
  local copies, waits for them, and re-layouts  3.11 us (3%)
    pallas_call x1, Pallas kernels, body(): pl.pallas_call(functools.partial(kernel, n_dev, n_all), out_shape=jax.Sha...  92.4 us
    unnamed x1, local copies, waits for them, and re-layouts  3.11 us

profile of v2, /device:TPU:1, one launch (start us, length us, event | category | flops | bytes accessed | tf_op | source)
XLA Modules:
  0.0 95.5 jit_solution(5198296386049154023)
XLA Ops:
  0.0 92.4 %butterfly.1 = f32[2,64,4096]{2,1,0:T(8,128)} custom-call(s32[2,64]{1,0:T(2,128)} %node_ref.1, s32[1,16]{1,0:T(1,128)} %bitcast.1, f32[2,64,4096]{2,1,0:T(8,128)} %w_hbm.1, bf16[128,256]{1,0:T(8,128)(2,1)} %constant.10.clone.t1_hbm, bf16[256,192]{1,0:T(8,128)(2,1)} %constant.11.clone.t3_hbm, bf16[2,256,64]{2,1,0:T(8,128)(2,1)} %constant.12.clone.tf_hbm, ...), custom_call_target="tpu_custom_call" | custom-call | tf_op jit(solution)/shard_map/butterfly/pallas_call | solution.py:591
  92.4 3.1 %copy.10 = f32[2,64,4096]{2,1,0:T(8,128)} copy(f32[2,64,4096]{2,1,0:T(8,128)} %butterfly.1) | data formatting | bytes 4194304

commit v3 on v2

--- a/solution.py
+++ b/solution.py
@@ -160,7 +160,6 @@
 
 
 ROWS = 32
-BLOCKS = [(r, l) for l in range(0, 256, 128) for r in range(0, 64, ROWS)]
 MESH = pl.DeviceIdType.MESH
 
 
@@ -194,10 +193,10 @@
     return dot(numbers, owner, NT_DIMS)[0:1, :], owner
 
 
-def kernel(n_dev, n_all, node_ref, owner_ref, w_hbm, t1_hbm, t3_hbm, tf_hbm, off_hbm, off3_hbm,
+def kernel(n_dev, n_all, n_group, node_ref, owner_ref, w_hbm, t1_hbm, t3_hbm, tf_hbm, off_hbm, off3_hbm,
            o_ref, x_ref, t1_ref, t3_ref, tf_ref, off_ref, off3_ref, z_ref, y_ref, tab1, tab2,
            tabm, tab3i, tab3o, tab4i, tabf, part, doff, t1s, xh, xl, y1, y2, wmat, x3, v4, tmat,
-           yy, send1, recv1, send2, recv2, local):
+           yy, send1, recv1, send2, recv2, local, ready):
     flat = lax.axis_index("grp") * n_dev + lax.axis_index("dev")
     h = lax.div(flat, 16)
     ry = lax.rem(flat, 16)
@@ -209,27 +208,34 @@
 
     barrier = pltpu.get_barrier_semaphore()
 
-    def greet(i, carry):
-        pl.semaphore_signal(barrier, inc=1, device_id=place(lax.rem(flat + i, n_all)),
-                            device_id_type=MESH)
-        return carry
-
-    lax.fori_loop(1, n_all, greet, 0)
-    pl.semaphore_wait(barrier, n_all - 1)
-
-    def chunk(m):
-        return w_hbm.at[:, :, pl.ds(pl.multiple_of(m * 256, 256), 256)]
-
-    def exchange1(i):
-        m = lax.rem(ry + i, 16)
+    def tell(semaphore, device):
+        pl.semaphore_signal(semaphore, inc=1, device_id=place(device), device_id_type=MESH)
+
+    for i in range(1, 16):
+        tell(barrier, h * 16 + lax.rem(ry + i, 16))
+    for g in range(1, n_group):
+        tell(barrier, lax.rem(h + g, n_group) * 16 + ry)
+    pl.semaphore_wait(barrier, 14 + n_group)
+    for g in range(1, n_group):
+        tell(ready, lax.rem(h + g, n_group) * 16 + ry)
+
+    def chunk(m, b):
+        return w_hbm.at[:, :, pl.ds(pl.multiple_of(m * 256 + b * 128, 128), 128)]
+
+    def exchange1(b, i):
+        m = (lax.rem(lax.div(ry, 8) + i // 8, 2) * 8
+             + lax.rem(lax.div(lax.rem(ry, 8), 2) + i // 2 % 4, 4) * 2 + lax.rem(ry + i, 2))
         return pltpu.make_async_remote_copy(
-            src_ref=chunk(m), dst_ref=x_ref.at[ry], send_sem=send1.at[i], recv_sem=recv1.at[i],
-            device_id=place(h * 16 + m), device_id_type=MESH)
-
-    for i in range(1, 16):
-        exchange1(i).start()
-    own1 = pltpu.make_async_copy(chunk(ry), x_ref.at[ry], recv1.at[0])
-    own1.start()
+            src_ref=chunk(m, b), dst_ref=x_ref.at[b, ry], send_sem=send1.at[b * 16 + i],
+            recv_sem=recv1.at[b * 16 + i], device_id=place(h * 16 + m), device_id_type=MESH)
+
+    for b in range(2):
+        for i in range(1, 16):
+            exchange1(b, i).start()
+    own1 = [pltpu.make_async_copy(chunk(ry, b), x_ref.at[b, ry], recv1.at[b * 16])
+            for b in range(2)]
+    for copy in own1:
+        copy.start()
     loads = [pltpu.make_async_copy(a, b, local.at[i]) for i, (a, b) in enumerate(
         [(t1_hbm, t1_ref), (t3_hbm, t3_ref), (tf_hbm, tf_ref), (off_hbm, off_ref),
          (off3_hbm, off3_ref)])]
@@ -334,21 +340,15 @@
     n = fiota((1, 128), 1)
     nrow = fiota((128, 16), 0)
     column, owner = columns_of(owner_ref, 2 * lax.div(nrow, 16) + lax.rem(nrow, 2))
-    erow = fiota((256, 16), 0)
-    picks = (lax.rem(lax.div(erow, 4), 16) == fiota((256, 16), 1)).astype(F32).astype(BF16)
+    erow = fiota((128, 16), 0)
+    picks = (lax.rem(lax.div(erow, 4), 16) == fiota((128, 16), 1)).astype(F32).astype(BF16)
     wcol = dot(picks, owner, NT_DIMS)
-    wlane = fiota((256, 128), 0)
-    digit = lax.rem(lax.div(wlane, 2), 2) + 2 * lax.div(wlane, 128)
-    wu = lax.rem(lax.div(fiota((256, 128), 1), 2), 8)
-    for v2d in range(4):
-        keep = jnp.where(digit == v2d, wcol, 0.0)
-
-        def fill(u8, carry):
-            wmat[pl.ds(pl.multiple_of(u8 * 256, 256), 256), v2d * 128:(v2d + 1) * 128] = jnp.where(
-                wu == u8, keep, 0.0).astype(BF16)
-            return carry
-
-        lax.fori_loop(0, 8, fill, 0)
+    wu = lax.rem(lax.div(fiota((128, 128), 1), 2), 8)
+    for v in range(2):
+        keep = jnp.where(lax.rem(lax.div(fiota((128, 128), 0), 2), 2) == v, wcol, 0.0)
+        for u in range(8):
+            wmat[u * 128:(u + 1) * 128, v * 128:(v + 1) * 128] = jnp.where(
+                wu == u, keep, 0.0).astype(BF16)
 
     u8 = lax.rem(lax.div(n, 2), 8)
 
@@ -409,114 +409,138 @@
 
     lax.fori_loop(0, 8, level4, 0)
 
-    own1.wait()
-    for i in range(1, 16):
-        exchange1(i).wait()
-
-    def turned(source, tab, index):
-        for c in range(4):
-            for r, l in BLOCKS:
-                rows = slice(r, r + ROWS)
-                re, im = source(c, rows, l)
-                parts = turn(re, im, tab, index(c), rows, slice(l, l + 128))
-                for p in range(2):
-                    hi, lo = split(parts[p])
-                    at = slice(c * 64 + r, c * 64 + r + ROWS)
-                    to = slice(p * 256 + l, p * 256 + l + 128)
-                    xh[at, to] = hi
-                    xl[at, to] = lo
-
-    def mixed(table):
-        first = dot(table[...], xh[...])
-        return first[:64] + first[64:] + dot(table[0:64], xl[...])
-
-    def run1(i, carry):
-        u2 = lax.rem(i, 4)
-        u1 = lax.div(i, 4)
-
-        def source(c, rows, l):
-            lanes = slice(l, l + 128)
-            return x_ref[u2 * 4 + c, 0, rows, lanes], x_ref[u2 * 4 + c, 1, rows, lanes]
-
-        turned(source, tab1, lambda c: (u1 * 4 + c) * 4 + u2)
-        y1[u1 * 4 + u2] = mixed(t1s)
-        return carry
-
-    lax.fori_loop(0, 16, run1, 0)
-
-    def run2(u, carry):
-        u1 = lax.rem(u, 4)
-        u2 = lax.div(u, 4)
-
-        def source(c, rows, l):
-            return (y1[u1 * 4 + c, rows, l:l + 128], y1[u1 * 4 + c, rows, 256 + l:384 + l])
-
-        turned(source, tab2, lambda c: (u1 * 4 + c) * 4 + u2)
-        out = mixed(t1_ref)
-        at = pl.multiple_of(lax.rem(u, 8) * 256, 256)
-        half = lax.div(u, 8)
-        for r, l in BLOCKS:
-            rows = slice(r, r + ROWS)
-            parts = turn(out[rows, l:l + 128], out[rows, 256 + l:384 + l], tabm, u, rows,
-                         slice(l, l + 128))
-            for p in range(2):
-                hi, lo = split(parts[p])
-                y2[half, p * 64 + r:p * 64 + r + ROWS, pl.ds(at + l, 128)] = hi
-                y2[half, 128 + p * 64 + r:128 + p * 64 + r + ROWS, pl.ds(at + l, 128)] = lo
-        return carry
-
-    lax.fori_loop(0, 16, run2, 0)
-
-    def run3(half, carry):
-        both = dot(y2[half], wmat[...])
-        summed = both[:128] + both[128:]
-        for v in range(4):
-            for r in range(0, 64, ROWS):
-                rows = slice(r, r + ROWS)
-                l = v * 128
-                parts = turn(summed[r:r + ROWS, l:l + 128],
-                             summed[64 + r:64 + r + ROWS, l:l + 128], tab3i, half * 4 + v, rows,
-                             slice(0, 128))
-                for p in range(2):
-                    hi, lo = split(parts[p])
-                    to = slice((v * 2 + p) * 128, (v * 2 + p + 1) * 128)
-                    x3[r:r + ROWS, to] = hi
-                    x3[64 + r:64 + r + ROWS, to] = lo
-                    x3[128 + r:128 + r + ROWS, to] = hi
-        for j in range(4):
-            out = dot(t3_ref[j * 64:(j + 1) * 64], x3[...])
-            for r in range(0, 64, ROWS):
-                rows = slice(r, r + ROWS)
-                re = None
-                for v in range(4):
-                    l = v * 256
-                    a, b = turn(out[rows, l:l + 128], out[rows, l + 128:l + 256], tab3o,
-                                (half * 4 + j) * 4 + v, rows, slice(0, 128))
-                    re = a if re is None else re + a
-                    im = b if v == 0 else im + b
-                re, im = turn(re, im, tab4i, half * 4 + j, rows, slice(0, 128))
-                v4[r:r + ROWS] = re
-                v4[64 + r:64 + r + ROWS] = im
-            flipped = v4[...].T
-            for k in range(8):
-                z_ref[k, j, pl.ds(pl.multiple_of(half * 16, 16), 16), :] = flipped[k * 16:(k + 1) * 16]
-        return carry
-
-    lax.fori_loop(0, 2, run3, 0)
-
-    def exchange2(i):
-        to = lax.rem(flat + i, n_all)
-        return pltpu.make_async_remote_copy(
-            src_ref=z_ref.at[lax.div(to, 16), lax.rem(to, 4)], dst_ref=y_ref.at[flat],
-            send_sem=send2, recv_sem=recv2.at[h], device_id=place(to), device_id_type=MESH)
-
-    def send(i, carry):
-        exchange2(i).start()
-        return carry
-
-    lax.fori_loop(1, n_all, send, 0)
-    own2 = pltpu.make_async_copy(z_ref.at[h, lax.rem(flat, 4)], y_ref.at[flat], recv2.at[h])
-    own2.start()
+    y0 = 2 * lax.rem(lax.div(flat, n_all // 4), 2) + lax.div(flat, n_all // 2)
+    x0 = lax.rem(lax.div(flat, 8), 4)
+    z0 = lax.rem(lax.div(flat, 2), 4)
+    c0 = lax.rem(flat, 2)
+
+    def send_half(half):
+        for odd in (1, 0):
+
+            def send(e, carry):
+                dz = lax.rem(e, 4)
+                dx = lax.rem(lax.div(e, 4) + dz, 4)
+                dy = 2 * lax.rem(lax.div(e, 16), 2) + odd
+                yy0 = lax.rem(y0 + dy, 4)
+                v = (lax.rem(x0 + dx, 4) * 8 + lax.rem(z0 + dz, 4) * 2
+                     + lax.rem(c0 + lax.div(e, 32), 2))
+                to = lax.rem(yy0, 2) * 64 + lax.div(yy0, 2) * 32 + v
+                pltpu.make_async_remote_copy(
+                    src_ref=z_ref.at[half, lax.div(to, 16), lax.rem(v, 4)],
+                    dst_ref=y_ref.at[flat, half], send_sem=send2, recv_sem=recv2.at[h],
+                    device_id=place(to), device_id_type=MESH).start()
+                return carry
+
+            lax.fori_loop(1 - odd, 64, send, 0)
+        pltpu.make_async_copy(z_ref.at[half, h, lax.rem(flat, 4)], y_ref.at[flat, half],
+                              recv2.at[h]).start()
+
+    def stage(b):
+        at = slice(b * 128, b * 128 + 128)
+        whole = slice(0, 128)
+
+        def turned(slot, source, tab, index):
+            for c in range(4):
+                for r in range(0, 64, ROWS):
+                    rows = slice(r, r + ROWS)
+                    re, im = source(c, rows)
+                    parts = turn(re, im, tab, index(c), rows, at)
+                    for p in range(2):
+                        hi, lo = split(parts[p])
+                        xh[slot, c * 64 + r:c * 64 + r + ROWS, p * 128:p * 128 + 128] = hi
+                        xl[slot, c * 64 + r:c * 64 + r + ROWS, p * 128:p * 128 + 128] = lo
+
+        def mixed(slot, table):
+            first = dot(table[...], xh[slot])
+            return first[:64] + first[64:] + dot(table[0:64], xl[slot])
+
+        def run1(u2, carry):
+            for u1 in range(4):
+                turned(u1, lambda c, rows: (x_ref[b, u2 * 4 + c, 0, rows],
+                                            x_ref[b, u2 * 4 + c, 1, rows]),
+                       tab1, lambda c: (u1 * 4 + c) * 4 + u2)
+                y1[u1 * 4 + u2] = mixed(u1, t1s)
+            return carry
+
+        lax.fori_loop(0, 4, run1, 0)
+
+        def run2(half, pair):
+            for slot in range(4):
+                u1 = 2 * pair + slot // 2
+                u2 = 2 * half + slot % 2
+                u = u1 + 4 * u2
+                turned(slot, lambda c, rows: (y1[u1 * 4 + c, rows, 0:128],
+                                              y1[u1 * 4 + c, rows, 128:256]),
+                       tab2, lambda c: (u1 * 4 + c) * 4 + u2)
+                out = mixed(slot, t1_ref)
+                to = pl.ds(pl.multiple_of((u1 + 4 * (slot % 2)) * 128, 128), 128)
+                for r in range(0, 64, ROWS):
+                    rows = slice(r, r + ROWS)
+                    parts = turn(out[rows, 0:128], out[rows, 128:256], tabm, u, rows, at)
+                    for p in range(2):
+                        hi, lo = split(parts[p])
+                        y2[p * 64 + r:p * 64 + r + ROWS, to] = hi
+                        y2[128 + p * 64 + r:128 + p * 64 + r + ROWS, to] = lo
+
+        def run3(half):
+            both = dot(y2[...], wmat[...])
+            summed = both[:128] + both[128:]
+            for v in range(2):
+                for r in range(0, 64, ROWS):
+                    rows = slice(r, r + ROWS)
+                    l = v * 128
+                    parts = turn(summed[r:r + ROWS, l:l + 128],
+                                 summed[64 + r:64 + r + ROWS, l:l + 128], tab3i,
+                                 half * 4 + 2 * b + v, rows, whole)
+                    for p in range(2):
+                        hi, lo = split(parts[p])
+                        to = slice((v * 2 + p) * 128, (v * 2 + p + 1) * 128)
+                        x3[r:r + ROWS, to] = hi
+                        x3[64 + r:64 + r + ROWS, to] = lo
+                        x3[128 + r:128 + r + ROWS, to] = hi
+            for j in range(4):
+                out = dot(t3_ref[j * 64:(j + 1) * 64], x3[...])
+                for r in range(0, 64, ROWS):
+                    rows = slice(r, r + ROWS)
+                    low = slice(64 + r, 64 + r + ROWS)
+                    if b == 1:
+                        re, im = v4[half * 4 + j, rows], v4[half * 4 + j, low]
+                    for v in range(2):
+                        l = v * 256
+                        p, q = turn(out[rows, l:l + 128], out[rows, l + 128:l + 256], tab3o,
+                                    (half * 4 + j) * 4 + 2 * b + v, rows, whole)
+                        first = b == 0 and v == 0
+                        re = p if first else re + p
+                        im = q if first else im + q
+                    if b == 1:
+                        re, im = turn(re, im, tab4i, half * 4 + j, rows, whole)
+                    v4[half * 4 + j, rows] = re
+                    v4[half * 4 + j, low] = im
+                if b == 1:
+                    flipped = v4[half * 4 + j].T
+                    for k in range(8):
+                        z_ref[half, k, j] = flipped[k * 16:(k + 1) * 16]
+
+        def run(half, carry):
+            def pairs(pair, carry):
+                run2(half, pair)
+                return carry
+
+            lax.fori_loop(0, 2, pairs, 0)
+            run3(half)
+            if b == 1:
+                send_half(half)
+            return carry
+
+        lax.fori_loop(0, 2, run, 0)
+
+    for b in range(2):
+        own1[b].wait()
+        for i in range(1, 16):
+            exchange1(b, i).wait()
+        if b == 1:
+            pl.semaphore_wait(ready, n_group - 1)
+        stage(b)
 
     v1d = lax.rem(ry, 4)
     v2d = lax.div(ry, 4)
@@ -555,11 +579,12 @@
 
     lax.fori_loop(0, 8, level5, 0)
 
-    def run4(src, carry):
+    def run4(e, carry):
+        src = lax.rem(lax.div(h, 4) + 1 + lax.div(e, 4), 2) * 4 + lax.rem(h + e, 4)
         landed = y_ref.at[pl.ds(pl.multiple_of(src * 16, 16), 16)]
         pltpu.make_async_copy(landed, landed, recv2.at[src]).wait()
         for m in range(16):
-            yy[pl.ds(m, 32, stride=16), :] = y_ref[src * 16 + m]
+            yy[pl.ds(m, 32, stride=16), :] = y_ref[src * 16 + m].reshape(32, 128)
         hi, lo = split(yy[...])
         out = dot(tmat[...], jnp.concatenate([hi, lo], axis=1), NT_DIMS)
         out = out[:128] + out[128:]
@@ -589,19 +614,19 @@
     hbm = pl.BlockSpec(memory_space=pl.ANY)
     dma = pltpu.SemaphoreType.DMA
     return pl.pallas_call(
-        functools.partial(kernel, n_dev, n_all),
+        functools.partial(kernel, n_dev, n_all, n_all // 16),
         out_shape=jax.ShapeDtypeStruct((2, 64, 4096), F32),
         in_specs=[vmem] * 2 + [hbm] * 6,
         out_specs=vmem,
         scratch_shapes=[
-            pltpu.VMEM((16, 2, 64, 256), F32),
+            pltpu.VMEM((2, 16, 2, 64, 128), F32),
             pltpu.VMEM(t1.shape, BF16),
             pltpu.VMEM(t3.shape, BF16),
             pltpu.VMEM(tf.shape, BF16),
             pltpu.VMEM(off.shape, F32),
             pltpu.VMEM(off3.shape, BF16),
-            pltpu.VMEM((8, 4, 32, 128), F32),
-            pltpu.VMEM((128, 32, 128), F32),
+            pltpu.VMEM((2, 8, 4, 16, 128), F32),
+            pltpu.VMEM((128, 2, 16, 128), F32),
             pltpu.VMEM((64, 2, 64, 256), F32),
             pltpu.VMEM((64, 2, 64, 256), F32),
             pltpu.VMEM((16, 2, 64, 256), F32),
@@ -612,20 +637,21 @@
             pltpu.VMEM((64, 256), F32),
             pltpu.VMEM((2, 64, 128), F32),
             pltpu.VMEM((128, 256), BF16),
-            pltpu.VMEM((256, 512), BF16),
-            pltpu.VMEM((256, 512), BF16),
-            pltpu.VMEM((16, 64, 512), F32),
-            pltpu.VMEM((2, 256, 2048), BF16),
-            pltpu.VMEM((2048, 512), BF16),
-            pltpu.VMEM((192, 1024), BF16),
-            pltpu.VMEM((128, 128), F32),
+            pltpu.VMEM((4, 256, 256), BF16),
+            pltpu.VMEM((4, 256, 256), BF16),
+            pltpu.VMEM((16, 64, 256), F32),
+            pltpu.VMEM((256, 1024), BF16),
+            pltpu.VMEM((1024, 256), BF16),
+            pltpu.VMEM((192, 512), BF16),
+            pltpu.VMEM((8, 128, 128), F32),
             pltpu.VMEM((256, 256), BF16),
             pltpu.VMEM((512, 128), F32),
-            dma((16,)),
-            dma((16,)),
+            dma((32,)),
+            dma((32,)),
             dma(()),
             dma((8,)),
             dma((5,)),
+            pltpu.SemaphoreType.REGULAR,
         ],
         compiler_params=pltpu.CompilerParams(
             vmem_limit_bytes=VMEM_LIMIT, collective_id=0, has_side_effects=True),

time: 95.7 us -> 75.7 us (0.79)
  Pallas kernels: 92.4 us -> 72.4 us
    pallas_call x1, Pallas kernels: 92.4 us -> 72.4 us  [body(): pl.pallas_call(functools.partial(kernel, n_dev, n_all, n_all // 16), out_...]
where the time goes in v3:
time: 75.7 us; the launch traced here: 75.5 us
  Pallas kernels  72.4 us (96%)
  local copies, waits for them, and re-layouts  3.11 us (4%)
    pallas_call x1, Pallas kernels, body(): pl.pallas_call(functools.partial(kernel, n_dev, n_all, n_all // 16), out_...  72.4 us
    unnamed x1, local copies, waits for them, and re-layouts  3.11 us

profile of v3, /device:TPU:1, one launch (start us, length us, event | category | flops | bytes accessed | tf_op | source)
XLA Modules:
  0.0 75.5 jit_solution(14753906557200253340)
XLA Ops:
  0.0 72.4 %butterfly.1 = f32[2,64,4096]{2,1,0:T(8,128)} custom-call(s32[2,64]{1,0:T(2,128)} %node_ref.1, s32[1,16]{1,0:T(1,128)} %bitcast.1, f32[2,64,4096]{2,1,0:T(8,128)} %w_hbm.1, bf16[128,256]{1,0:T(8,128)(2,1)} %constant.10.clone.t1_hbm, bf16[256,192]{1,0:T(8,128)(2,1)} %constant.11.clone.t3_hbm, bf16[2,256,64]{2,1,0:T(8,128)(2,1)} %constant.12.clone.tf_hbm, ...), custom_call_target="tpu_custom_call" | custom-call | tf_op jit(solution)/shard_map/butterfly/pallas_call | solution.py:616
  72.4 3.1 %copy.10 = f32[2,64,4096]{2,1,0:T(8,128)} copy(f32[2,64,4096]{2,1,0:T(8,128)} %butterfly.1) | data formatting | bytes 4194304

commit v4 on v3

--- a/solution.py
+++ b/solution.py
@@ -136,7 +136,8 @@
 def freq_columns(d1, d2, a1, a2, v1, v2):
     e1 = v1 * d1
     e2 = v2 * d2
-    return 2.0 * e1, 2.0 * e2, e1 * d1 + e2 * d2, a1 * d1 + a2 * d2
+    linear = a2 * d2 if isinstance(a1, float) and a1 == 0.0 else a1 * d1 + a2 * d2
+    return 2.0 * e1, 2.0 * e2, e1 * d1 + e2 * d2, linear
 
 
 def freq_row(g1, g2, v1, v2):
@@ -195,7 +196,7 @@
 
 def kernel(n_dev, n_all, n_group, node_ref, owner_ref, w_hbm, t1_hbm, t3_hbm, tf_hbm, off_hbm, off3_hbm,
            o_ref, x_ref, t1_ref, t3_ref, tf_ref, off_ref, off3_ref, z_ref, y_ref, tab1, tab2,
-           tabm, tab3i, tab3o, tab4i, tabf, part, doff, t1s, xh, xl, y1, y2, wmat, x3, v4, tmat,
+           tabm, tab3i, tab3o, tab4i, tabf, lin2, line, prod, part, doff, t1s, xh, xl, y1, y2, wmat, x3, v4, tmat,
            yy, send1, recv1, send2, recv2, local, ready):
     flat = lax.axis_index("grp") * n_dev + lax.axis_index("dev")
     h = lax.div(flat, 16)
@@ -254,6 +255,31 @@
     bx = [tofloat(lax.rem(v, 64)) for v in lane]
     by = [4.0 * ryf + tofloat(lax.div(v, 64)) for v in lane]
 
+    def products(index, offsets, scale, shift, width, child):
+        for l in range(0, 256, 128):
+            for axis, at in ((0, bx[l // 128]), (1, by[l // 128])):
+                g = width * at + child - HALF
+                for r in range(0, 64, ROWS):
+                    d = scale * offsets[axis, r:r + ROWS] + shift
+                    prod[axis, index, r:r + ROWS, l:l + 128] = d * (2.0 * g + d)
+
+    def products1(i, carry):
+        child = tofloat(lax.div(i, 2))
+        products(i, doff, 16.0, 16.0 * (child - 0.5), 64.0, 32.0 * (tofloat(lax.rem(i, 2)) + 0.5))
+        return carry
+
+    def products2(i, carry):
+        products(4 + i, off_ref, 32.0, 32.0 * (tofloat(i) - 0.5), 64.0, 32.0)
+        products(6 + i, off_ref, 32.0, 0.0, 64.0, 32.0 * (tofloat(i) + 0.5))
+        return carry
+
+    lax.fori_loop(0, 4, products1, 0)
+
+    def freq_rest(row, ix, iy, v1, v2, rows, lanes):
+        square, base = row
+        numer = v1 * prod[0, ix, rows, lanes] + v2 * prod[1, iy, rows, lanes]
+        return numer / (root(square + numer) + base)
+
     def level1(i, carry):
         c = lax.rem(i, 4)
         u1 = lax.div(i, 4)
@@ -262,62 +288,95 @@
         v1, v2 = speeds(splat(a1), splat(a2))
         sx = 16.0 * (tofloat(bit(c, 0)) - 0.5)
         sy = 16.0 * (tofloat(bit(c, 1)) - 0.5)
-        cols = [freq_columns(sx + 16.0 * doff[0, r:r + ROWS], sy + 16.0 * doff[1, r:r + ROWS],
-                             -a1, -a2, v1, v2) for r in range(0, 64, ROWS)]
+        for r in range(0, 64, ROWS):
+            line[r:r + ROWS] = -(a1 * (sx + 16.0 * doff[0, r:r + ROWS])
+                                 + a2 * (sy + 16.0 * doff[1, r:r + ROWS]))
 
         def inner(u2, carry):
             for l in range(0, 256, 128):
                 k = l // 128
                 row = freq_row(32.0 * (2.0 * bx[k] + tofloat(bit(u2, 0)) + 0.5) - HALF,
                                32.0 * (2.0 * by[k] + tofloat(bit(u2, 1)) + 0.5) - HALF, v1, v2)
-                g1, g2, square, base = row
                 for r in range(0, 64, ROWS):
-                    e1, e2, e0, linear = cols[r // ROWS]
-                    numer = e1 * g1 + e2 * g2 + e0
-                    cycles = linear - numer / (root(square + numer) + base)
-                    save(tab1, i * 4 + u2, cycles, slice(r, r + ROWS), slice(l, l + 128))
+                    rows = slice(r, r + ROWS)
+                    lanes = slice(l, l + 128)
+                    rest = freq_rest(row[2:], 2 * bit(c, 0) + bit(u2, 0),
+                                     2 * bit(c, 1) + bit(u2, 1), v1, v2, rows, lanes)
+                    save(tab1, i * 4 + u2, line[rows] - rest, rows, lanes)
             return carry
 
-        lax.fori_loop(0, 4, inner, 0)
+        lax.fori_loop(0, 4, inner, 0, unroll=2)
         return carry
 
     lax.fori_loop(0, 16, level1, 0)
 
+    lax.fori_loop(0, 2, products2, 0)
+    def linear2(i, carry):
+        ux = tofloat(lax.div(i, 2))
+        a1 = (2.0 * hf + ux + 0.5) / 32.0
+        b1 = (4.0 * hf + 2.0 * ux + tofloat(lax.rem(i, 2)) + 0.5) / 64.0
+        for r in range(0, 64, ROWS):
+            rows = slice(r, r + ROWS)
+            o = off_ref[0, rows]
+            save(lin2, i, 32.0 * (a1 * o - b1 * (o - 0.5)), rows, slice(0, 128))
+        return carry
+
+    lax.fori_loop(0, 4, linear2, 0)
+
+    mirror = fiota((ROWS, 128), 1)
+    mirror = lax.div(mirror, 64) * 64 + 63 - lax.rem(mirror, 64)
+
+    def mirrored(tab, index, other, cycles, lin, which, r, lanes):
+        cs, sn = trig(cycles)
+        cl = lin[which, 0, r:r + ROWS]
+        sl = lin[which, 1, r:r + ROWS]
+        p, q, s, t = cs * cl, sn * sl, sn * cl, cs * sl
+        tab[index, 0, r:r + ROWS, lanes] = p - q
+        tab[index, 1, r:r + ROWS, lanes] = s + t
+        for part_id, value in enumerate((p + q, s - t)):
+            value = jnp.take_along_axis(value, mirror, axis=1, mode="promise_in_bounds")
+            for k in range(0, ROWS, 8):
+                to = 56 - r - k
+                tab[other, part_id, to:to + 8, lanes] = value[k:k + 8]
+
     def level2(i, carry):
-        c = lax.rem(i, 4)
-        u1 = lax.div(i, 4)
+        u1 = lax.div(i, 2)
         a1 = (2.0 * hf + tofloat(bit(u1, 0)) + 0.5) / 32.0
         a2 = (tofloat(bit(u1, 1)) + 0.5) / 32.0
         v1, v2 = speeds(splat(a1), splat(a2))
-        cx = tofloat(bit(c, 0))
-        cy = tofloat(bit(c, 1))
-        for l in range(0, 256, 128):
-            k = l // 128
-            row = freq_row(32.0 * (2.0 * bx[k] + cx + 0.5) - HALF,
-                           32.0 * (2.0 * by[k] + cy + 0.5) - HALF, v1, v2)
-            for r in range(0, 64, ROWS):
-                cols = freq_columns(32.0 * off_ref[0, r:r + ROWS], 32.0 * off_ref[1, r:r + ROWS],
-                                    a1, a2, v1, v2)
-                part[r:r + ROWS, l:l + 128] = freq_cycles(cols, row)
+        cy = tofloat(lax.rem(i, 2))
+        cyi = lax.rem(i, 2)
+        for r in range(0, 64, ROWS):
+            rows = slice(r, r + ROWS)
+            for l in range(0, 256, 128):
+                k = l // 128
+                lanes = slice(l, l + 128)
+                row = freq_row(32.0 * (2.0 * bx[k] + 0.5) - HALF,
+                               32.0 * (2.0 * by[k] + cy + 0.5) - HALF, v1, v2)
+                part[rows, lanes] = (a2 * (32.0 * off_ref[1, rows])
+                                     + freq_rest(row[2:], 6, 6 + cyi, v1, v2, rows, lanes))
+        index = (u1 * 4 + 2 * cyi) * 4
 
         def inner(u2, carry):
             b1 = (4.0 * hf + 2.0 * tofloat(bit(u1, 0)) + tofloat(bit(u2, 0)) + 0.5) / 64.0
             b2 = (2.0 * tofloat(bit(u1, 1)) + tofloat(bit(u2, 1)) + 0.5) / 64.0
             w1, w2 = speeds(splat(b1), splat(b2))
-            rows = [freq_row(64.0 * (bx[k] + 0.5) - HALF, 64.0 * (by[k] + 0.5) - HALF, w1, w2)
-                    for k in range(2)]
-            for r in range(0, 64, ROWS):
-                cols = freq_columns(32.0 * (off_ref[0, r:r + ROWS] + (cx - 0.5)),
-                                    32.0 * (off_ref[1, r:r + ROWS] + (cy - 0.5)), b1, b2, w1, w2)
-                for l in range(0, 256, 128):
-                    cycles = part[r:r + ROWS, l:l + 128] - freq_cycles(cols, rows[l // 128])
-                    save(tab2, i * 4 + u2, cycles, slice(r, r + ROWS), slice(l, l + 128))
+            for l in range(0, 256, 128):
+                k = l // 128
+                lanes = slice(l, l + 128)
+                row = freq_row(64.0 * (bx[k] + 0.5) - HALF, 64.0 * (by[k] + 0.5) - HALF, w1, w2)
+                for r in range(0, 64, ROWS):
+                    rows = slice(r, r + ROWS)
+                    rest = freq_rest(row[2:], 4, 4 + cyi, w1, w2, rows, lanes)
+                    down = (b2 * 32.0) * (off_ref[1, rows] + (cy - 0.5))
+                    mirrored(tab2, index + u2, index + 4 + u2, part[rows, lanes] - down - rest,
+                             lin2, bit(u1, 0) * 2 + bit(u2, 0), r, lanes)
             return carry
 
-        lax.fori_loop(0, 4, inner, 0)
-        return carry
-
-    lax.fori_loop(0, 16, level2, 0)
+        lax.fori_loop(0, 4, inner, 0, unroll=2)
+        return carry
+
+    lax.fori_loop(0, 8, level2, 0)
 
     def middle(u, carry):
         u1 = lax.rem(u, 4)
@@ -335,7 +394,7 @@
                      slice(l, l + 128))
         return carry
 
-    lax.fori_loop(0, 16, middle, 0)
+    lax.fori_loop(0, 16, middle, 0, unroll=2)
 
     n = fiota((1, 128), 1)
     nrow = fiota((128, 16), 0)
@@ -634,6 +693,9 @@
             pltpu.VMEM((32, 2, 64, 128), F32),
             pltpu.VMEM((8, 2, 64, 128), F32),
             pltpu.VMEM((8, 2, 64, 512), F32),
+            pltpu.VMEM((4, 2, 64, 128), F32),
+            pltpu.VMEM((64, 128), F32),
+            pltpu.VMEM((2, 8, 64, 256), F32),
             pltpu.VMEM((64, 256), F32),
             pltpu.VMEM((2, 64, 128), F32),
             pltpu.VMEM((128, 256), BF16),

time: 75.7 us -> 71.9 us (0.950)
  Pallas kernels: 72.4 us -> 68.6 us
    pallas_call x1, Pallas kernels: 72.4 us -> 68.6 us  [body(): pl.pallas_call(functools.partial(kernel, n_dev, n_all, n_all // 16), out_...]
where the time goes in v4:
time: 71.9 us; the launch traced here: 71.7 us
  Pallas kernels  68.6 us (95%)
  local copies, waits for them, and re-layouts  3.11 us (4%)
    pallas_call x1, Pallas kernels, body(): pl.pallas_call(functools.partial(kernel, n_dev, n_all, n_all // 16), out_...  68.6 us
    unnamed x1, local copies, waits for them, and re-layouts  3.11 us

profile of v4, /device:TPU:1, one launch (start us, length us, event | category | flops | bytes accessed | tf_op | source)
XLA Modules:
  0.0 71.7 jit_solution(147545423999648867)
XLA Ops:
  0.0 68.6 %butterfly.1 = f32[2,64,4096]{2,1,0:T(8,128)} custom-call(s32[2,64]{1,0:T(2,128)} %node_ref.1, s32[1,16]{1,0:T(1,128)} %bitcast.1, f32[2,64,4096]{2,1,0:T(8,128)} %w_hbm.1, bf16[128,256]{1,0:T(8,128)(2,1)} %constant.10.clone.t1_hbm, bf16[256,192]{1,0:T(8,128)(2,1)} %constant.11.clone.t3_hbm, bf16[2,256,64]{2,1,0:T(8,128)(2,1)} %constant.12.clone.tf_hbm, ...), custom_call_target="tpu_custom_call" | custom-call | tf_op jit(solution)/shard_map/butterfly/pallas_call | solution.py:675
  68.6 3.1 %copy.10 = f32[2,64,4096]{2,1,0:T(8,128)} copy(f32[2,64,4096]{2,1,0:T(8,128)} %butterfly.1) | data formatting | bytes 4194304

commit v5 on v4

--- a/solution.py
+++ b/solution.py
@@ -216,6 +216,78 @@
         tell(barrier, h * 16 + lax.rem(ry + i, 16))
     for g in range(1, n_group):
         tell(barrier, lax.rem(h + g, n_group) * 16 + ry)
+    loads = [pltpu.make_async_copy(a, b, local.at[i]) for i, (a, b) in enumerate(
+        [(t1_hbm, t1_ref), (t3_hbm, t3_ref), (tf_hbm, tf_ref), (off_hbm, off_ref),
+         (off3_hbm, off3_ref)])]
+    for load in loads:
+        load.start()
+    for load in loads:
+        load.wait()
+
+    onehot = node_onehot(node_ref)
+    for axis in range(2):
+        doff[axis] = sum(dot(onehot, off3_ref[p, axis], TN_DIMS) for p in (2, 1, 0))
+    for c in range(4):
+        t1s[:, c * 64:(c + 1) * 64] = dot(t1_ref[:, c * 64:(c + 1) * 64], onehot).astype(BF16)
+
+    lane = [fiota((1, 128), 1) + k for k in (0, 128)]
+    bx = [tofloat(lax.rem(v, 64)) for v in lane]
+    by = [4.0 * ryf + tofloat(lax.div(v, 64)) for v in lane]
+
+    def products(index, offsets, scale, shift, width, child):
+        for l in range(0, 256, 128):
+            for axis, at in ((0, bx[l // 128]), (1, by[l // 128])):
+                g = width * at + child - HALF
+                for r in range(0, 64, ROWS):
+                    d = scale * offsets[axis, r:r + ROWS] + shift
+                    prod[axis, index, r:r + ROWS, l:l + 128] = d * (2.0 * g + d)
+
+    def products1(i, carry):
+        child = tofloat(lax.div(i, 2))
+        products(i, doff, 16.0, 16.0 * (child - 0.5), 64.0, 32.0 * (tofloat(lax.rem(i, 2)) + 0.5))
+        return carry
+
+    def products2(i, carry):
+        products(4 + i, off_ref, 32.0, 32.0 * (tofloat(i) - 0.5), 64.0, 32.0)
+        products(6 + i, off_ref, 32.0, 0.0, 64.0, 32.0 * (tofloat(i) + 0.5))
+        return carry
+
+    lax.fori_loop(0, 4, products1, 0)
+    lax.fori_loop(0, 2, products2, 0)
+
+    def linear2(i, carry):
+        ux = tofloat(lax.div(i, 2))
+        a1 = (2.0 * hf + ux + 0.5) / 32.0
+        b1 = (4.0 * hf + 2.0 * ux + tofloat(lax.rem(i, 2)) + 0.5) / 64.0
+        for r in range(0, 64, ROWS):
+            rows = slice(r, r + ROWS)
+            o = off_ref[0, rows]
+            save(lin2, i, 32.0 * (a1 * o - b1 * (o - 0.5)), rows, slice(0, 128))
+        return carry
+
+    lax.fori_loop(0, 4, linear2, 0)
+
+    n = fiota((1, 128), 1)
+    nrow = fiota((128, 16), 0)
+    column, owner = columns_of(owner_ref, 2 * lax.div(nrow, 16) + lax.rem(nrow, 2))
+    erow = fiota((128, 16), 0)
+    picks = (lax.rem(lax.div(erow, 4), 16) == fiota((128, 16), 1)).astype(F32).astype(BF16)
+    wcol = dot(picks, owner, NT_DIMS)
+    wu = lax.rem(lax.div(fiota((128, 128), 1), 2), 8)
+    for v in range(2):
+        keep = jnp.where(lax.rem(lax.div(fiota((128, 128), 0), 2), 2) == v, wcol, 0.0)
+        for u in range(8):
+            wmat[u * 128:(u + 1) * 128, v * 128:(v + 1) * 128] = jnp.where(
+                wu == u, keep, 0.0).astype(BF16)
+
+    u8 = lax.rem(lax.div(n, 2), 8)
+
+    def parent(u):
+        u1 = lax.rem(u, 4)
+        u2 = lax.div(u, 4)
+        return (tofloat(2 * lax.rem(u1, 2) + lax.rem(u2, 2)),
+                tofloat(2 * lax.div(u1, 2) + lax.div(u2, 2)))
+
     pl.semaphore_wait(barrier, 14 + n_group)
     for g in range(1, n_group):
         tell(ready, lax.rem(h + g, n_group) * 16 + ry)
@@ -237,43 +309,6 @@
             for b in range(2)]
     for copy in own1:
         copy.start()
-    loads = [pltpu.make_async_copy(a, b, local.at[i]) for i, (a, b) in enumerate(
-        [(t1_hbm, t1_ref), (t3_hbm, t3_ref), (tf_hbm, tf_ref), (off_hbm, off_ref),
-         (off3_hbm, off3_ref)])]
-    for load in loads:
-        load.start()
-    for load in loads:
-        load.wait()
-
-    onehot = node_onehot(node_ref)
-    for axis in range(2):
-        doff[axis] = sum(dot(onehot, off3_ref[p, axis], TN_DIMS) for p in (2, 1, 0))
-    for c in range(4):
-        t1s[:, c * 64:(c + 1) * 64] = dot(t1_ref[:, c * 64:(c + 1) * 64], onehot).astype(BF16)
-
-    lane = [fiota((1, 128), 1) + k for k in (0, 128)]
-    bx = [tofloat(lax.rem(v, 64)) for v in lane]
-    by = [4.0 * ryf + tofloat(lax.div(v, 64)) for v in lane]
-
-    def products(index, offsets, scale, shift, width, child):
-        for l in range(0, 256, 128):
-            for axis, at in ((0, bx[l // 128]), (1, by[l // 128])):
-                g = width * at + child - HALF
-                for r in range(0, 64, ROWS):
-                    d = scale * offsets[axis, r:r + ROWS] + shift
-                    prod[axis, index, r:r + ROWS, l:l + 128] = d * (2.0 * g + d)
-
-    def products1(i, carry):
-        child = tofloat(lax.div(i, 2))
-        products(i, doff, 16.0, 16.0 * (child - 0.5), 64.0, 32.0 * (tofloat(lax.rem(i, 2)) + 0.5))
-        return carry
-
-    def products2(i, carry):
-        products(4 + i, off_ref, 32.0, 32.0 * (tofloat(i) - 0.5), 64.0, 32.0)
-        products(6 + i, off_ref, 32.0, 0.0, 64.0, 32.0 * (tofloat(i) + 0.5))
-        return carry
-
-    lax.fori_loop(0, 4, products1, 0)
 
     def freq_rest(row, ix, iy, v1, v2, rows, lanes):
         square, base = row
@@ -309,19 +344,6 @@
         return carry
 
     lax.fori_loop(0, 16, level1, 0)
-
-    lax.fori_loop(0, 2, products2, 0)
-    def linear2(i, carry):
-        ux = tofloat(lax.div(i, 2))
-        a1 = (2.0 * hf + ux + 0.5) / 32.0
-        b1 = (4.0 * hf + 2.0 * ux + tofloat(lax.rem(i, 2)) + 0.5) / 64.0
-        for r in range(0, 64, ROWS):
-            rows = slice(r, r + ROWS)
-            o = off_ref[0, rows]
-            save(lin2, i, 32.0 * (a1 * o - b1 * (o - 0.5)), rows, slice(0, 128))
-        return carry
-
-    lax.fori_loop(0, 4, linear2, 0)
 
     mirror = fiota((ROWS, 128), 1)
     mirror = lax.div(mirror, 64) * 64 + 63 - lax.rem(mirror, 64)
@@ -395,27 +417,6 @@
         return carry
 
     lax.fori_loop(0, 16, middle, 0, unroll=2)
-
-    n = fiota((1, 128), 1)
-    nrow = fiota((128, 16), 0)
-    column, owner = columns_of(owner_ref, 2 * lax.div(nrow, 16) + lax.rem(nrow, 2))
-    erow = fiota((128, 16), 0)
-    picks = (lax.rem(lax.div(erow, 4), 16) == fiota((128, 16), 1)).astype(F32).astype(BF16)
-    wcol = dot(picks, owner, NT_DIMS)
-    wu = lax.rem(lax.div(fiota((128, 128), 1), 2), 8)
-    for v in range(2):
-        keep = jnp.where(lax.rem(lax.div(fiota((128, 128), 0), 2), 2) == v, wcol, 0.0)
-        for u in range(8):
-            wmat[u * 128:(u + 1) * 128, v * 128:(v + 1) * 128] = jnp.where(
-                wu == u, keep, 0.0).astype(BF16)
-
-    u8 = lax.rem(lax.div(n, 2), 8)
-
-    def parent(u):
-        u1 = lax.rem(u, 4)
-        u2 = lax.div(u, 4)
-        return (tofloat(2 * lax.rem(u1, 2) + lax.rem(u2, 2)),
-                tofloat(2 * lax.div(u1, 2) + lax.div(u2, 2)))
 
     def level3(half, carry):
         mx, my = parent(u8 + 8 * half)
@@ -486,13 +487,14 @@
                 to = lax.rem(yy0, 2) * 64 + lax.div(yy0, 2) * 32 + v
                 pltpu.make_async_remote_copy(
                     src_ref=z_ref.at[half, lax.div(to, 16), lax.rem(v, 4)],
-                    dst_ref=y_ref.at[flat, half], send_sem=send2, recv_sem=recv2.at[h],
+                    dst_ref=y_ref.at[half, flat], send_sem=send2,
+                    recv_sem=recv2.at[half * 8 + h],
                     device_id=place(to), device_id_type=MESH).start()
                 return carry
 
             lax.fori_loop(1 - odd, 64, send, 0)
-        pltpu.make_async_copy(z_ref.at[half, h, lax.rem(flat, 4)], y_ref.at[flat, half],
-                              recv2.at[h]).start()
+        pltpu.make_async_copy(z_ref.at[half, h, lax.rem(flat, 4)], y_ref.at[half, flat],
+                              recv2.at[half * 8 + h]).start()
 
     def stage(b):
         at = slice(b * 128, b * 128 + 128)
@@ -513,7 +515,16 @@
             first = dot(table[...], xh[slot])
             return first[:64] + first[64:] + dot(table[0:64], xl[slot])
 
-        def run1(u2, carry):
+        def run1(e, carry):
+            ux = lax.rem(lax.div(ry, 8) + lax.div(e, 2), 2)
+            uz = lax.rem(lax.div(ry, 4) + e, 2)
+            u2 = 2 * ux + uz
+            for c in range(4):
+                i = (lax.rem(lax.div(ry, 8) + ux, 2) * 8
+                     + lax.rem(lax.div(lax.rem(ry, 8), 2) + 4 - 2 * uz - c // 2, 4) * 2
+                     + lax.rem(ry + c, 2))
+                landed = x_ref.at[b, u2 * 4 + c]
+                pltpu.make_async_copy(landed, landed, recv1.at[b * 16 + i]).wait()
             for u1 in range(4):
                 turned(u1, lambda c, rows: (x_ref[b, u2 * 4 + c, 0, rows],
                                             x_ref[b, u2 * 4 + c, 1, rows]),
@@ -594,9 +605,6 @@
         lax.fori_loop(0, 2, run, 0)
 
     for b in range(2):
-        own1[b].wait()
-        for i in range(1, 16):
-            exchange1(b, i).wait()
         if b == 1:
             pl.semaphore_wait(ready, n_group - 1)
         stage(b)
@@ -639,30 +647,35 @@
     lax.fori_loop(0, 8, level5, 0)
 
     def run4(e, carry):
-        src = lax.rem(lax.div(h, 4) + 1 + lax.div(e, 4), 2) * 4 + lax.rem(h + e, 4)
-        landed = y_ref.at[pl.ds(pl.multiple_of(src * 16, 16), 16)]
-        pltpu.make_async_copy(landed, landed, recv2.at[src]).wait()
+        half = lax.div(e, 8)
+        src = lax.rem(lax.div(h, 4) + 1 + lax.rem(lax.div(e, 4), 2), 2) * 4 + lax.rem(h + e, 4)
+        landed = y_ref.at[half, pl.ds(pl.multiple_of(src * 16, 16), 16)]
+        pltpu.make_async_copy(landed, landed, recv2.at[half * 8 + src]).wait()
         for m in range(16):
-            yy[pl.ds(m, 32, stride=16), :] = y_ref[src * 16 + m].reshape(32, 128)
+            yy[pl.ds(m, 16, stride=16), :] = y_ref[half, src * 16 + m]
         hi, lo = split(yy[...])
         out = dot(tmat[...], jnp.concatenate([hi, lo], axis=1), NT_DIMS)
         out = out[:128] + out[128:]
-        for l in range(0, 512, 128):
-            lanes = pl.ds(pl.multiple_of(src * 512 + l, 128), 128)
+        for l in range(0, 256, 128):
+            there = pl.ds(pl.multiple_of(half * 256 + l, 128), 128)
+            lanes = pl.ds(pl.multiple_of(src * 512 + half * 256 + l, 128), 128)
             for r in range(0, 64, ROWS):
                 rows = slice(r, r + ROWS)
                 re, im = turn(out[r:r + ROWS, l:l + 128], out[64 + r:64 + r + ROWS, l:l + 128],
-                              tabf, src, rows, slice(l, l + 128))
+                              tabf, src, rows, there)
                 o_ref[0, rows, lanes] = re
                 o_ref[1, rows, lanes] = im
         return carry
 
-    lax.fori_loop(0, 8, run4, 0)
-    sent = y_ref.at[pl.ds(0, n_all - 1)]
+    lax.fori_loop(0, 16, run4, 0)
+    sent = y_ref.at[:, pl.ds(0, n_all - 1)]
     pltpu.make_async_copy(sent, sent, send2).wait()
-
-
-VMEM_LIMIT = 62 * 1024 * 1024
+    for b in range(2):
+        for i in range(1, 16):
+            exchange1(b, i).wait_send()
+
+
+VMEM_LIMIT = 60 * 1024 * 1024
 
 
 def body(weights, owner_map, node_index):
@@ -670,11 +683,11 @@
     n_dev = lax.axis_size("dev")
     n_all = lax.axis_size("grp") * n_dev
     vmem = pl.BlockSpec(memory_space=pltpu.VMEM)
-    hbm = pl.BlockSpec(memory_space=pl.ANY)
+    hbm = pl.BlockSpec(memory_space=pltpu.HBM)
     dma = pltpu.SemaphoreType.DMA
     return pl.pallas_call(
         functools.partial(kernel, n_dev, n_all, n_all // 16),
-        out_shape=jax.ShapeDtypeStruct((2, 64, 4096), F32),
+        out_shape=pltpu.VMEM((2, 64, 4096), F32),
         in_specs=[vmem] * 2 + [hbm] * 6,
         out_specs=vmem,
         scratch_shapes=[
@@ -685,7 +698,7 @@
             pltpu.VMEM(off.shape, F32),
             pltpu.VMEM(off3.shape, BF16),
             pltpu.VMEM((2, 8, 4, 16, 128), F32),
-            pltpu.VMEM((128, 2, 16, 128), F32),
+            pltpu.VMEM((2, 128, 16, 128), F32),
             pltpu.VMEM((64, 2, 64, 256), F32),
             pltpu.VMEM((64, 2, 64, 256), F32),
             pltpu.VMEM((16, 2, 64, 256), F32),
@@ -707,11 +720,11 @@
             pltpu.VMEM((192, 512), BF16),
             pltpu.VMEM((8, 128, 128), F32),
             pltpu.VMEM((256, 256), BF16),
-            pltpu.VMEM((512, 128), F32),
+            pltpu.VMEM((256, 128), F32),
             dma((32,)),
             dma((32,)),
             dma(()),
-            dma((8,)),
+            dma((16,)),
             dma((5,)),
             pltpu.SemaphoreType.REGULAR,
         ],

time: 71.9 us -> 67.2 us (0.935)
  Pallas kernels: 68.6 us -> 65.7 us
  local copies, waits for them, and re-layouts: 3.11 us -> 1.32 us
    pallas_call x1, Pallas kernels: 68.6 us -> 65.7 us  [body(): pl.pallas_call(functools.partial(kernel, n_dev, n_all, n_all // 16), out_...]
    unnamed x1, local copies, waits for them, and re-layouts: 3.11 us -> 1.32 us
where the time goes in v5:
time: 67.2 us; the launch traced here: 67 us
  Pallas kernels  65.7 us (98%)
  local copies, waits for them, and re-layouts  1.32 us (2%)
    pallas_call x1, Pallas kernels, body(): pl.pallas_call(functools.partial(kernel, n_dev, n_all, n_all // 16), out_...  65.7 us

profile of v5, /device:TPU:1, one launch (start us, length us, event | category | flops | bytes accessed | tf_op | source)
XLA Modules:
  0.0 67.0 jit_solution(12451973044125504728)
XLA Ops:
  0.0 65.7 %butterfly.1 = f32[2,64,4096]{2,1,0:T(8,128)S(1)} custom-call(s32[2,64]{1,0:T(2,128)} %node_ref.1, s32[1,16]{1,0:T(1,128)} %bitcast.1, f32[2,64,4096]{2,1,0:T(8,128)} %w_hbm.1, bf16[128,256]{1,0:T(8,128)(2,1)} %constant.10.clone.t1_hbm, bf16[256,192]{1,0:T(8,128)(2,1)} %constant.11.clone.t3_hbm, bf16[2,256,64]{2,1,0:T(8,128)(2,1)} %constant.12.clone.tf_hbm, ...), custom_call_target="tpu_custom_call" | custom-call | tf_op jit(solution)/shard_map/butterfly/pallas_call | solution.py:688
  65.7 1.3 %copy.10 = f32[2,64,4096]{2,1,0:T(8,128)} copy(f32[2,64,4096]{2,1,0:T(8,128)S(1)} %butterfly.1) | data formatting | bytes 4194304

commit v6 on v5

--- a/solution.py
+++ b/solution.py
@@ -195,9 +195,10 @@
 
 
 def kernel(n_dev, n_all, n_group, node_ref, owner_ref, w_hbm, t1_hbm, t3_hbm, tf_hbm, off_hbm, off3_hbm,
-           o_ref, x_ref, t1_ref, t3_ref, tf_ref, off_ref, off3_ref, z_ref, y_ref, tab1, tab2,
+           o_ref, e_ref, x_ref, t1_ref, t3_ref, tf_ref, off_ref, off3_ref, z_ref, y_ref, tab1, tab2,
            tabm, tab3i, tab3o, tab4i, tabf, lin2, line, prod, part, doff, t1s, xh, xl, y1, y2, wmat, x3, v4, tmat,
-           yy, send1, recv1, send2, recv2, local, ready):
+           yy, send1, recv1, sea, ea, seb, eb, sec, ec, sxa,
+           xa, sxb, xb, local, ready):
     flat = lax.axis_index("grp") * n_dev + lax.axis_index("dev")
     h = lax.div(flat, 16)
     ry = lax.rem(flat, 16)
@@ -469,32 +470,87 @@
 
     lax.fori_loop(0, 8, level4, 0)
 
-    y0 = 2 * lax.rem(lax.div(flat, n_all // 4), 2) + lax.div(flat, n_all // 2)
+    yi = lax.div(flat, 32)
     x0 = lax.rem(lax.div(flat, 8), 4)
-    z0 = lax.rem(lax.div(flat, 2), 4)
-    c0 = lax.rem(flat, 2)
+    zc = lax.rem(flat, 8)
+    z0 = lax.div(zc, 2)
+    c0 = lax.rem(zc, 2)
+    x1 = x0 + 1 - 2 * lax.rem(x0, 2)
+
+    def at_device(y, x, m):
+        return place(y * 32 + x * 8 + m)
+
+    def near(x, o):
+        return 3 - x if o else x
+
+    def remote(source, target, sender, receiver, device):
+        return pltpu.make_async_remote_copy(
+            src_ref=source, dst_ref=target, send_sem=sender, recv_sem=receiver,
+            device_id=device, device_id_type=MESH)
+
+    def arrive(ref, semaphore):
+        pltpu.make_async_copy(ref, ref, semaphore).wait()
+
+    pairs_of = [(t, o) for t in (2, 1, 3, 0) for o in (1, 0)]
+
+    def spread(d):
+        return lax.rem(z0 + d // 2, 4) * 2 + lax.rem(c0 + d, 2)
+
+    def e_first():
+        for t, o in pairs_of:
+            yk = lax.rem(yi + t, 4)
+            xk = near(x0, o)
+            block = z_ref.at[0, yk * 2 + lax.div(xk, 2)]
+            s = o * 4 + t
+            if s == 0:
+                pltpu.make_async_copy(block, e_ref.at[yi, x0], ea.at[s]).start()
+            else:
+                remote(block, e_ref.at[yi, x0], sea.at[s], ea.at[s],
+                       at_device(yk, xk, zc)).start()
+
+    def x_first():
+        for t, o in pairs_of:
+            yk = lax.rem(yi + t, 4)
+            xk = near(x0, o)
+            k = yk * 2 + lax.div(xk, 2)
+            s = o * 4 + t
+            for d in (4, 5, 2, 3, 6, 7, 0, 1):
+                m = spread(d)
+                block = z_ref.at[1, k, lax.rem(m, 4)]
+                if s == 0 and d == 0:
+                    pltpu.make_async_copy(block, y_ref.at[1, yi, x0, zc], xa.at[s]).start()
+                else:
+                    remote(block, y_ref.at[1, yi, x0, zc], sxa.at[s], xa.at[s],
+                           at_device(yk, xk, m)).start()
+
+    def e_pass():
+        for t, o in pairs_of:
+            s = o * 4 + t
+            block = e_ref.at[lax.rem(yi + 4 - t, 4), near(x0, o)]
+            arrive(block, ea.at[s])
+            remote(block, block, seb.at[s], eb.at[s], at_device(yi, x1, zc)).start()
+
+    def x_pass():
+        for t, o in pairs_of:
+            s = o * 4 + t
+            block = y_ref.at[1, lax.rem(yi + 4 - t, 4), near(x0, o)]
+            arrive(block, xa.at[s])
+            remote(block, block, sxb.at[s], xb.at[s], at_device(yi, x1, zc)).start()
+
+    def e_last(x, o):
+        xs = near(x, o)
+        for d in (4, 5, 2, 3, 6, 7, 1, 0):
+            m = spread(d)
+            block = e_ref.at[:, xs, lax.rem(m, 4)]
+            if d == 0:
+                pltpu.make_async_copy(block, y_ref.at[0, :, xs, zc], ec.at[xs]).start()
+            else:
+                remote(block, y_ref.at[0, :, xs, zc], sec, ec.at[xs],
+                       at_device(yi, x0, m)).start()
 
     def send_half(half):
-        for odd in (1, 0):
-
-            def send(e, carry):
-                dz = lax.rem(e, 4)
-                dx = lax.rem(lax.div(e, 4) + dz, 4)
-                dy = 2 * lax.rem(lax.div(e, 16), 2) + odd
-                yy0 = lax.rem(y0 + dy, 4)
-                v = (lax.rem(x0 + dx, 4) * 8 + lax.rem(z0 + dz, 4) * 2
-                     + lax.rem(c0 + lax.div(e, 32), 2))
-                to = lax.rem(yy0, 2) * 64 + lax.div(yy0, 2) * 32 + v
-                pltpu.make_async_remote_copy(
-                    src_ref=z_ref.at[half, lax.div(to, 16), lax.rem(v, 4)],
-                    dst_ref=y_ref.at[half, flat], send_sem=send2,
-                    recv_sem=recv2.at[half * 8 + h],
-                    device_id=place(to), device_id_type=MESH).start()
-                return carry
-
-            lax.fori_loop(1 - odd, 64, send, 0)
-        pltpu.make_async_copy(z_ref.at[half, h, lax.rem(flat, 4)], y_ref.at[half, flat],
-                              recv2.at[half * 8 + h]).start()
+        pl.when(half == 0)(e_first)
+        pl.when(half == 1)(x_first)
 
     def stage(b):
         at = slice(b * 128, b * 128 + 128)
@@ -609,6 +665,15 @@
             pl.semaphore_wait(ready, n_group - 1)
         stage(b)
 
+    e_pass()
+    e_last(x0, 0)
+    e_last(x0, 1)
+    x_pass()
+    for o in range(2):
+        for t in (2, 1, 3, 0):
+            arrive(e_ref.at[lax.rem(yi + 4 - t, 4), near(x1, o)], eb.at[o * 4 + t])
+        e_last(x1, o)
+
     v1d = lax.rem(ry, 4)
     v2d = lax.div(ry, 4)
     zero = jnp.zeros((64, 64), BF16)
@@ -646,18 +711,15 @@
 
     lax.fori_loop(0, 8, level5, 0)
 
-    def run4(e, carry):
-        half = lax.div(e, 8)
-        src = lax.rem(lax.div(h, 4) + 1 + lax.rem(lax.div(e, 4), 2), 2) * 4 + lax.rem(h + e, 4)
-        landed = y_ref.at[half, pl.ds(pl.multiple_of(src * 16, 16), 16)]
-        pltpu.make_async_copy(landed, landed, recv2.at[half * 8 + src]).wait()
+    def run4(half, src):
         for m in range(16):
-            yy[pl.ds(m, 16, stride=16), :] = y_ref[half, src * 16 + m]
+            yy[pl.ds(m, 16, stride=16), :] = y_ref[half, lax.div(src, 2),
+                                                  lax.rem(src, 2) * 2 + m // 8, m % 8]
         hi, lo = split(yy[...])
         out = dot(tmat[...], jnp.concatenate([hi, lo], axis=1), NT_DIMS)
         out = out[:128] + out[128:]
         for l in range(0, 256, 128):
-            there = pl.ds(pl.multiple_of(half * 256 + l, 128), 128)
+            there = slice(half * 256 + l, half * 256 + l + 128)
             lanes = pl.ds(pl.multiple_of(src * 512 + half * 256 + l, 128), 128)
             for r in range(0, 64, ROWS):
                 rows = slice(r, r + ROWS)
@@ -665,11 +727,33 @@
                               tabf, src, rows, there)
                 o_ref[0, rows, lanes] = re
                 o_ref[1, rows, lanes] = im
-        return carry
-
-    lax.fori_loop(0, 16, run4, 0)
-    sent = y_ref.at[:, pl.ds(0, n_all - 1)]
-    pltpu.make_async_copy(sent, sent, send2).wait()
+
+    for o in range(2):
+        pair = lax.div(near(x0, o), 2)
+
+        def half1(t, carry):
+            ys = lax.rem(yi + 4 - t, 4)
+            arrive(y_ref.at[1, ys, near(x1, o)], xb.at[o * 4 + t])
+            run4(1, ys * 2 + pair)
+            return carry
+
+        def half0(ys, carry):
+            run4(0, ys * 2 + pair)
+            return carry
+
+        lax.fori_loop(0, 4, half1, 0)
+        for x in (x0, x1):
+            arrive(y_ref.at[0, :, near(x, o)], ec.at[near(x, o)])
+        lax.fori_loop(0, 4, half0, 0)
+    sent = y_ref.at[0, :, :, pl.ds(0, 7)]
+    arrive(sent, sec)
+    for s in range(8):
+        if s > 0:
+            arrive(e_ref.at[0, 0], sea.at[s])
+            arrive(y_ref.at[1, 0, 0], sxa.at[s])
+        arrive(e_ref.at[0, 0], seb.at[s])
+        arrive(y_ref.at[1, 0, 0], sxb.at[s])
+    arrive(y_ref.at[1, 0, 0, pl.ds(0, 7)], sxa.at[0])
     for b in range(2):
         for i in range(1, 16):
             exchange1(b, i).wait_send()
@@ -691,6 +775,7 @@
         in_specs=[vmem] * 2 + [hbm] * 6,
         out_specs=vmem,
         scratch_shapes=[
+            pltpu.VMEM((4, 4, 4, 16, 128), F32),
             pltpu.VMEM((2, 16, 2, 64, 128), F32),
             pltpu.VMEM(t1.shape, BF16),
             pltpu.VMEM(t3.shape, BF16),
@@ -698,7 +783,7 @@
             pltpu.VMEM(off.shape, F32),
             pltpu.VMEM(off3.shape, BF16),
             pltpu.VMEM((2, 8, 4, 16, 128), F32),
-            pltpu.VMEM((2, 128, 16, 128), F32),
+            pltpu.VMEM((2, 4, 4, 8, 16, 128), F32),
             pltpu.VMEM((64, 2, 64, 256), F32),
             pltpu.VMEM((64, 2, 64, 256), F32),
             pltpu.VMEM((16, 2, 64, 256), F32),
@@ -723,8 +808,16 @@
             pltpu.VMEM((256, 128), F32),
             dma((32,)),
             dma((32,)),
+            dma((8,)),
+            dma((8,)),
+            dma((8,)),
+            dma((8,)),
             dma(()),
-            dma((16,)),
+            dma((4,)),
+            dma((8,)),
+            dma((8,)),
+            dma((8,)),
+            dma((8,)),
             dma((5,)),
             pltpu.SemaphoreType.REGULAR,
         ],

time: 67.2 us -> 65.9 us (0.981)
  Pallas kernels: 65.7 us -> 64.4 us
    pallas_call x1, Pallas kernels: 65.7 us -> 64.4 us  [body(): pl.pallas_call(functools.partial(kernel, n_dev, n_all, n_all // 16), out_...]
where the time goes in v6:
time: 65.9 us; the launch traced here: 65.7 us
  Pallas kernels  64.4 us (98%)
  local copies, waits for them, and re-layouts  1.32 us (2%)
    pallas_call x1, Pallas kernels, body(): pl.pallas_call(functools.partial(kernel, n_dev, n_all, n_all // 16), out_...  64.4 us
    unnamed x1, local copies, waits for them, and re-layouts  1.32 us

profile of v6, /device:TPU:1, one launch (start us, length us, event | category | flops | bytes accessed | tf_op | source)
XLA Modules:
  0.0 65.7 jit_solution(5858952522510743628)
XLA Ops:
  0.0 64.4 %butterfly.1 = f32[2,64,4096]{2,1,0:T(8,128)S(1)} custom-call(s32[2,64]{1,0:T(2,128)} %node_ref.1, s32[1,16]{1,0:T(1,128)} %bitcast.1, f32[2,64,4096]{2,1,0:T(8,128)} %w_hbm.1, bf16[128,256]{1,0:T(8,128)(2,1)} %constant.10.clone.t1_hbm, bf16[256,192]{1,0:T(8,128)(2,1)} %constant.11.clone.t3_hbm, bf16[2,256,64]{2,1,0:T(8,128)(2,1)} %constant.12.clone.tf_hbm, ...), custom_call_target="tpu_custom_call" | custom-call | tf_op jit(solution)/shard_map/butterfly/pallas_call | solution.py:772
  64.4 1.3 %copy.10 = f32[2,64,4096]{2,1,0:T(8,128)} copy(f32[2,64,4096]{2,1,0:T(8,128)S(1)} %butterfly.1) | data formatting | bytes 4194304

commit v7 on v6

--- a/solution.py
+++ b/solution.py
@@ -491,7 +491,7 @@
     def arrive(ref, semaphore):
         pltpu.make_async_copy(ref, ref, semaphore).wait()
 
-    pairs_of = [(t, o) for t in (2, 1, 3, 0) for o in (1, 0)]
+    pairs_of = [(t, o) for t in (0, 1, 3, 2) for o in (0, 1)]
 
     def spread(d):
         return lax.rem(z0 + d // 2, 4) * 2 + lax.rem(c0 + d, 2)
@@ -670,7 +670,7 @@
     e_last(x0, 1)
     x_pass()
     for o in range(2):
-        for t in (2, 1, 3, 0):
+        for t in (0, 1, 3, 2):
             arrive(e_ref.at[lax.rem(yi + 4 - t, 4), near(x1, o)], eb.at[o * 4 + t])
         e_last(x1, o)
 

time: 65.9 us -> 64.4 us (0.977)
  Pallas kernels: 64.4 us -> 62.9 us
    pallas_call x1, Pallas kernels: 64.4 us -> 62.9 us  [body(): pl.pallas_call(functools.partial(kernel, n_dev, n_all, n_all // 16), out_...]
where the time goes in v7:
time: 64.4 us; the launch traced here: 64.3 us
  Pallas kernels  62.9 us (98%)
  local copies, waits for them, and re-layouts  1.32 us (2%)
    pallas_call x1, Pallas kernels, body(): pl.pallas_call(functools.partial(kernel, n_dev, n_all, n_all // 16), out_...  62.9 us
    unnamed x1, local copies, waits for them, and re-layouts  1.32 us

profile of v7, /device:TPU:1, one launch (start us, length us, event | category | flops | bytes accessed | tf_op | source)
XLA Modules:
  0.0 64.3 jit_solution(5385988436550249753)
XLA Ops:
  0.0 62.9 %butterfly.1 = f32[2,64,4096]{2,1,0:T(8,128)S(1)} custom-call(s32[2,64]{1,0:T(2,128)} %node_ref.1, s32[1,16]{1,0:T(1,128)} %bitcast.1, f32[2,64,4096]{2,1,0:T(8,128)} %w_hbm.1, bf16[128,256]{1,0:T(8,128)(2,1)} %constant.10.clone.t1_hbm, bf16[256,192]{1,0:T(8,128)(2,1)} %constant.11.clone.t3_hbm, bf16[2,256,64]{2,1,0:T(8,128)(2,1)} %constant.12.clone.tf_hbm, ...), custom_call_target="tpu_custom_call" | custom-call | tf_op jit(solution)/shard_map/butterfly/pallas_call | solution.py:772
  63.0 1.3 %copy.10 = f32[2,64,4096]{2,1,0:T(8,128)} copy(f32[2,64,4096]{2,1,0:T(8,128)S(1)} %butterfly.1) | data formatting | bytes 4194304

commit v8 on v7

--- a/solution.py
+++ b/solution.py
@@ -731,7 +731,8 @@
     for o in range(2):
         pair = lax.div(near(x0, o), 2)
 
-        def half1(t, carry):
+        def half1(e, carry):
+            t = e + lax.div(e, 2) - 2 * lax.div(e, 3)
             ys = lax.rem(yi + 4 - t, 4)
             arrive(y_ref.at[1, ys, near(x1, o)], xb.at[o * 4 + t])
             run4(1, ys * 2 + pair)

time: 64.4 us -> 64.2 us (level)
  no operation moved by 1% of the time
where the time goes in v8:
time: 64.2 us; the launch traced here: 64 us
  Pallas kernels  62.7 us (98%)
  local copies, waits for them, and re-layouts  1.32 us (2%)
    pallas_call x1, Pallas kernels, body(): pl.pallas_call(functools.partial(kernel, n_dev, n_all, n_all // 16), out_...  62.7 us
    unnamed x1, local copies, waits for them, and re-layouts  1.32 us

profile of v8, /device:TPU:1, one launch (start us, length us, event | category | flops | bytes accessed | tf_op | source)
XLA Modules:
  0.0 64.0 jit_solution(17540030060629796314)
XLA Ops:
  0.0 62.7 %butterfly.1 = f32[2,64,4096]{2,1,0:T(8,128)S(1)} custom-call(s32[2,64]{1,0:T(2,128)} %node_ref.1, s32[1,16]{1,0:T(1,128)} %bitcast.1, f32[2,64,4096]{2,1,0:T(8,128)} %w_hbm.1, bf16[128,256]{1,0:T(8,128)(2,1)} %constant.10.clone.t1_hbm, bf16[256,192]{1,0:T(8,128)(2,1)} %constant.11.clone.t3_hbm, bf16[2,256,64]{2,1,0:T(8,128)(2,1)} %constant.12.clone.tf_hbm, ...), custom_call_target="tpu_custom_call" | custom-call | tf_op jit(solution)/shard_map/butterfly/pallas_call | solution.py:773
  62.7 1.3 %copy.10 = f32[2,64,4096]{2,1,0:T(8,128)} copy(f32[2,64,4096]{2,1,0:T(8,128)S(1)} %butterfly.1) | data formatting | bytes 4194304
